TPU v7x, 512 devices: a whole 4x4x16 slice. The times are simulated.
512 devices in a mesh: space: 64 (over x_lo, z, core), chan: 8 (over y, x_hi).
Axes of the slice: x: 4 (x_hi: 2, x_lo: 2; x = x_hi * 2 + x_lo), y: 4, z: 16, core: 2. Of those that a mesh axis runs over, the one named last changes fastest.
Arguments:
- volume: bfloat16 [64, 64, 48, 128], P('chan', 'space'), may hold values from -6 to 6
- weight: bfloat16 [64, 64, 3, 3, 3], P('chan'), may hold values from -0.15625 to 0.15625
- bias: float32 [64], P('chan'), may hold values from -3 to 3
- upstream: bfloat16 [64, 64, 48, 128], P('chan', 'space'), may hold values from -6 to 6
Outputs:
- activated: bfloat16 [64, 64, 48, 128], P('chan', 'space')
- input_grad: bfloat16 [64, 64, 48, 128], P('chan', 'space')
- weight_grad: float32 [64, 64, 3, 3, 3], P('chan')
- bias_grad: float32 [64], P('chan')
All inputs are finite; a program needn't handle non-finite values.
Results may differ from a plain program's by a relative error of at most 0.008.
Values may be sent and summed in bfloat16 or wider, within the bound.
A program may use at most 64 MiB of HBM per device.

v0:
```python
import math

import jax
import jax.numpy as jnp
from jax import lax
from jax.sharding import PartitionSpec as P

leakage = 0.1


def padded(array, sides, width):
    for axis, dim in sides:
        count, length = (lax.axis_size(axis), array.shape[dim])
        up = [(i, (i + 1) % count) for i in range(count - 1)]
        down = [(j, i) for i, j in up]
        last = lax.slice_in_dim(array, length - width, length, axis=dim)
        first = lax.slice_in_dim(array, 0, width, axis=dim)
        before = lax.ppermute(last, axis, up)
        after = lax.ppermute(first, axis, down)
        array = jnp.concatenate([before, array, after], axis=dim)
    return array


def convolve(lhs, rhs, padding):
    return lax.conv_general_dilated(
        lhs,
        rhs,
        (1, 1, 1),
        padding,
        dimension_numbers=("NCDHW", "OIDHW", "NCDHW"),
        preferred_element_type=jnp.float32,
    )


def shards(volume, weight, bias, upstream):
    share = volume.shape[0]
    cells = lax.axis_size("space") * volume.shape[1] * volume.shape[2] * volume.shape[3]
    factor = 1.0 / math.sqrt(cells)
    filters_all = lax.all_gather(weight, "chan", axis=0, tiled=True)
    offset = lax.axis_index("chan") * share
    padding = [(0, 0), (1, 1), (1, 1)]
    allchan = lax.all_gather(volume, "chan", axis=0, tiled=True)
    rimmed = padded(allchan, (("space", 1),), 1)
    preact = convolve(rimmed[None], weight, padding)[0] + bias[:, None, None, None]
    activated = (leakage * preact + (1.0 - leakage) * jax.nn.softplus(preact)).astype(jnp.bfloat16)
    delta = (
        upstream.astype(jnp.float32) * (leakage + (1.0 - leakage) * jax.nn.sigmoid(preact))
    ).astype(jnp.bfloat16)
    delta_all = lax.all_gather(delta, "chan", axis=0, tiled=True)
    delta_rim = padded(delta_all, (("space", 1),), 1)
    selected = lax.dynamic_slice_in_dim(filters_all, offset, share, 1)
    flipped = jnp.transpose(selected, (1, 0, 2, 3, 4))[:, :, ::-1, ::-1, ::-1]
    input_grad = convolve(delta_rim[None], flipped, padding)[0].astype(jnp.bfloat16)
    partial_w = convolve(rimmed[:, None], delta[:, None], padding)
    partial_w = jnp.transpose(partial_w, (1, 0, 2, 3, 4))
    partial_b = jnp.sum(delta.astype(jnp.float32), axis=(1, 2, 3))
    summed_w, summed_b = lax.psum((partial_w, partial_b), "space")
    return (activated, input_grad, summed_w * factor, summed_b * factor)


def solution(mesh):
    placed = (
        P("chan", "space", None, None),
        P("chan", None, None, None, None),
        P("chan"),
        P("chan", "space", None, None),
    )
    return jax.shard_map(
        shards,
        mesh=mesh,
        in_specs=placed,
        out_specs=(
            P("chan", "space", None, None),
            P("chan", "space", None, None),
            P("chan", None, None, None, None),
            P("chan"),
        ),
        check_vma=False,
    )
```

profile of v0, /device:TPU:1, one launch (start us, length us, event | category | flops | bytes accessed | tf_op | source)
XLA Modules:
  0.0 494.8 jit_solution(5919151661601681311)
XLA Ops:
  0.6 35.8 %all_gather.9 = bf16[64,1,48,128]{3,2,1,0:T(8,128)(2,1)} all-gather(bf16[8,1,48,128]{3,2,1,0:T(8,128)(2,1)} %param.4), channel_id=1, replica_groups=mesh['space'=64,'chan'=8] {'chan'}, dimensions={0}, use_global_device_ids=true | all-gather | bytes 884736 | tf_op jit(solution)/shard_map/all_gather | solution.py:42
  36.4 12.6 %collective-permute-start.1 = (bf16[64,1,48,128]{3,2,1,0:T(8,128)(2,1)}, bf16[64,1,48,128]{3,2,1,0:T(8,128)(2,1)}, u32[]{:S(2)}, u32[]{:S(2)}) collective-permute-start(bf16[64,1,48,128]{3,2,1,0:T(8,128)(2,1)} %all_gather.9), channel_id=1, source_target_pairs={{8,0},{16,8},{24,16},{32,24},{40,32},{48,40},{56,48},{64,56},{72,6... | collective-permute-start | bytes 2359304 | tf_op jit(solution)/shard_map/ppermute | solution.py:19
  49.0 1.9 collective-permute-start
  50.9 2.3 copy.68
  53.2 1.8 copy.73
  54.9 36.8 %all_gather.11 = bf16[64,64,3,3,3]{1,0,4,3,2:T(8,128)(2,1)} all-gather(bf16[8,64,3,3,3]{1,0,4,3,2:T(8,128)(2,1)} %param.5), channel_id=1, replica_groups=mesh['space'=64,'chan'=8] {'chan'}, dimensions={0}, use_global_device_ids=true | all-gather | bytes 248832 | tf_op jit(solution)/shard_map/all_gather | solution.py:39
  91.7 0.0 collective-permute-done.1
  91.7 2.3 copy.69
  94.0 0.0 collective-permute-done
  94.0 3.1 copy.67
  97.1 4.3 fusion.20
  101.5 0.9 pad
  102.4 0.0 copy-start.1
  102.4 1.3 copy.71
  103.7 0.2 slice.4
  103.9 0.0 copy-done.1
  103.9 0.0 copy-start.2
  103.9 12.7 %fusion.6 = f32[1,48,8,17,8]{4,2,3,1,0:T(8,128)S(1)} fusion(bf16[8,64,3,3,3]{1,0,4,3,2:T(8,128)(2,1)S(1)} %copy-done.1, bf16[64,3,48,1,7,2]{0,4,5,2,1,3:T(8,128)(2,1)S(1)} %slice.4, bf16[64,3,48,1,8,17]{0,4,5,2,1,3:T(8,128)(2,1)S(1)} %copy.71), kind=kOutput, calls=%fused_computation.8 | convolution fusion | flops 186384384 | bytes 3001344 | tf_op jit(solution)/shard_map/conv_general_dilated | solution.py:25
  116.6 0.0 copy-start.3
  116.6 2.0 copy.72
  118.6 0.0 copy-done.2
  118.6 1.3 broadcast_select_fusion
  119.9 0.0 copy-done.3
  119.9 1.7 convert_reduce_fusion
  121.6 42.9 %all_gather.10 = bf16[64,1,48,128]{2,0,3,1:T(8,128)(2,1)S(1)} all-gather(bf16[8,1,48,128]{2,0,3,1:T(8,128)(2,1)S(1)} %get-tuple-element.23), channel_id=1, replica_groups=mesh['space'=64,'chan'=8] {'chan'}, dimensions={0}, use_global_device_ids=true | all-gather | bytes 884736 | tf_op jit(solution)/shard_map/all_gather | solution.py:49
  164.4 2.2 copy.74
  166.6 7.0 %collective-permute-start.3 = (bf16[64,1,48,128]{3,2,1,0:T(8,128)(2,1)S(1)}, bf16[64,1,48,128]{3,2,1,0:T(8,128)(2,1)}, u32[]{:S(2)}, u32[]{:S(2)}) collective-permute-start(bf16[64,1,48,128]{3,2,1,0:T(8,128)(2,1)S(1)} %copy.74), channel_id=1, source_target_pairs={{8,0},{16,8},{24,16},{32,24},{40,32},{48,40},{56,48},{64,56},{72,6... | collective-permute-start | bytes 2359304 | tf_op jit(solution)/shard_map/ppermute | solution.py:19
  173.6 1.9 collective-permute-start.2
  175.5 5.0 %copy.85 = bf16[8,1,1,48,128]{0,1,4,3,2:T(2,128)(2,1)} copy(bf16[8,1,1,48,128]{3,0,4,2,1:T(8,128)(2,1)S(1)} %bitcast.36) | data formatting | bytes 196608 | tf_op jit(solution)/shard_map/broadcast_in_dim | solution.py:54
  180.6 67.0 %fusion.2 = f32[8,64,3,3,3]{1,0,4,3,2:T(8,128)S(1)} fusion(bf16[8,1,1,48,128]{0,1,4,3,2:T(2,128)(2,1)} %copy.85, bf16[64,1,3,48,128]{0,3,4,2,1:T(8,128)(2,1)} %get-tuple-element.24), kind=kOutput, calls=%fused_computation.3 | convolution fusion | flops 166637568 | bytes 2512896 | tf_op jit(solution)/shard_map/transpose | solution.py:55
  247.6 0.8 copy.86
  248.4 204.6 %all-reduce = (f32[8,64,3,3,3]{1,0,4,3,2:T(8,128)S(1)}, f32[8]{0:T(128)S(1)}) all-reduce(f32[8,64,3,3,3]{1,0,4,3,2:T(8,128)S(1)} %fusion.2, f32[8]{0:T(128)S(1)} %get-tuple-element.22), channel_id=1, replica_groups=mesh['space'=64,'chan'=8] {'space'}, use_global_device_ids=true, to_apply=%region_0.1 | all-reduce | flops 13832 | bytes 110656 | tf_op jit(solution)/shard_map/psum | solution.py:57
  453.0 0.5 broadcast_multiply_fusion.1
  453.5 0.7 broadcast_multiply_fusion
  454.2 0.0 collective-permute-done.3
  454.2 4.7 copy.77
  458.9 0.0 collective-permute-done.2
  458.9 4.7 copy.76
  463.5 3.7 maximum_bitcast_fusion
  467.2 4.5 pad.2
  471.7 0.0 copy-start
  471.7 10.0 %copy.80 = bf16[64,3,48,1,8,17]{0,4,5,2,1,3:T(8,128)(2,1)} copy(bf16[64,3,48,1,8,17]{2,0,5,4,1,3:T(8,128)(2,1)} %bitcast.34) | data formatting | bytes 5013504 | tf_op jit(solution)/shard_map/conv_general_dilated | solution.py:25
  481.7 1.2 slice.6
  483.0 0.0 copy-done
  483.0 9.0 %fusion.10 = bf16[1,48,8,17,8]{4,2,3,1,0:T(8,128)(2,1)S(1)} fusion(bf16[64,3,48,1,7,2]{0,4,5,2,1,3:T(8,128)(2,1)S(1)} %slice.6, bf16[64,3,48,1,8,17]{0,4,5,2,1,3:T(8,128)(2,1)} %copy.80, bf16[64,64,3,3,3]{1,0,4,3,2:T(8,128)(2,1)S(1)} %copy-done, s32[]{:T(128)S(6)} %select_n.16), kind=kOutput, calls=%fused_computation.11 | convolution fusion | flops 186384384 | bytes 3090436 | tf_op jit(solution)/shard_map/conv_general_dilated | solution.py:25
  492.0 1.5 copy.82
  493.5 0.2 select_convert_fusion
  493.7 0.8 copy.87
  (1 shorter events, 0.0 us)
Async XLA Ops:
  36.4 55.3 %collective-permute-start.1 = (bf16[64,1,48,128]{3,2,1,0:T(8,128)(2,1)}, bf16[64,1,48,128]{3,2,1,0:T(8,128)(2,1)}, u32[]{:S(2)}, u32[]{:S(2)}) collective-permute-start(bf16[64,1,48,128]{3,2,1,0:T(8,128)(2,1)} %all_gather.9), channel_id=1, source_target_pairs={{8,0},{16,8},{24,16},{32,24},{40,32},{48,40},{56,48},{64,56},{72,6... | collective-permute-start | bytes 2359304 | tf_op jit(solution)/shard_map/ppermute | solution.py:19
  49.0 45.0 %collective-permute-start = (bf16[64,1,48,128]{3,2,1,0:T(8,128)(2,1)}, bf16[64,1,48,128]{3,2,1,0:T(8,128)(2,1)}, u32[]{:S(2)}, u32[]{:S(2)}) collective-permute-start(bf16[64,1,48,128]{3,2,1,0:T(8,128)(2,1)} %all_gather.9), channel_id=1, source_target_pairs={{0,8},{8,16},{16,24},{24,32},{32,40},{40,48},{48,56},{56,64},{64,7... | collective-permute-start | bytes 2359304 | tf_op jit(solution)/shard_map/ppermute | solution.py:18
  102.4 1.5 copy-start.1
  103.9 14.7 %copy-start.2 = (pred[8,17]{1,0:T(8,128)(4,1)S(1)}, pred[8,17]{1,0:T(8,128)(4,1)}, u32[]{:S(2)}) copy-start(pred[8,17]{1,0:T(8,128)(4,1)} %constant.33) | copy-start | bytes 412
  116.6 3.3 copy-start.3
  166.6 287.6 %collective-permute-start.3 = (bf16[64,1,48,128]{3,2,1,0:T(8,128)(2,1)S(1)}, bf16[64,1,48,128]{3,2,1,0:T(8,128)(2,1)}, u32[]{:S(2)}, u32[]{:S(2)}) collective-permute-start(bf16[64,1,48,128]{3,2,1,0:T(8,128)(2,1)S(1)} %copy.74), channel_id=1, source_target_pairs={{8,0},{16,8},{24,16},{32,24},{40,32},{48,40},{56,48},{64,56},{72,6... | collective-permute-start | bytes 2359304 | tf_op jit(solution)/shard_map/ppermute | solution.py:19
  173.6 285.3 %collective-permute-start.2 = (bf16[64,1,48,128]{3,2,1,0:T(8,128)(2,1)S(1)}, bf16[64,1,48,128]{3,2,1,0:T(8,128)(2,1)}, u32[]{:S(2)}, u32[]{:S(2)}) collective-permute-start(bf16[64,1,48,128]{3,2,1,0:T(8,128)(2,1)S(1)} %copy.74), channel_id=1, source_target_pairs={{0,8},{8,16},{16,24},{24,32},{32,40},{40,48},{48,56},{56,64},{64,7... | collective-permute-start | bytes 2359304 | tf_op jit(solution)/shard_map/ppermute | solution.py:18
  471.7 11.3 %copy-start = (bf16[64,64,3,3,3]{1,0,4,3,2:T(8,128)(2,1)S(1)}, bf16[64,64,3,3,3]{1,0,4,3,2:T(8,128)(2,1)}, u32[]{:S(2)}) copy-start(bf16[64,64,3,3,3]{1,0,4,3,2:T(8,128)(2,1)} %all_gather.11) | copy-start | bytes 663556
where the time goes:
time: 500 us; the launch traced here: 495 us
  blocking collectives  320 us (64%)
  matrix products  88.7 us (18%)
  local copies, waits for them, and re-layouts  49.2 us (10%)
  starting transfers between devices  23.4 us (5%)
  other arithmetic  12.4 us (2%)
    psum x1, blocking collectives, shards(): summed_w, summed_b = lax.psum((partial_w, partial_b), 'space')  205 us
    transpose x1, matrix products, shards(): partial_w = jnp.transpose(partial_w, (1, 0, 2, 3, 4))  67 us
    all_gather x1, blocking collectives, shards(): delta_all = lax.all_gather(delta, 'chan', axis=0, tiled=True)  42.9 us
    all_gather x1, blocking collectives, shards(): filters_all = lax.all_gather(weight, 'chan', axis=0, tiled=True)  36.8 us
    all_gather x1, blocking collectives, shards(): allchan = lax.all_gather(volume, 'chan', axis=0, tiled=True)  35.8 us
    conv_general_dilated x2, matrix products, convolve(): lax.conv_general_dilated(lhs, rhs, (1, 1, 1), padding, dimension_numbers=...  21.7 us
    ppermute x2, starting transfers between devices, padded(): after = lax.ppermute(first, axis, down)  19.5 us
    conv_general_dilated x6, local copies, waits for them, and re-layouts, convolve(): lax.conv_general_dilated(lhs, rhs, (1, 1, 1), padding, dimension_numbers=...  16.2 us
  transfers between devices with their start and end apart: 4, of which 0 were waited for; matrix products, arithmetic and copies ran while one was open for 17% of the time, Pallas kernels for 0%

commit v1 on v0

v1 whole, which is shorter than its diff:
```python
import functools
import math

import jax
import jax.numpy as jnp
from jax import lax
from jax.experimental import pallas as pl
from jax.experimental.pallas import tpu as pltpu
from jax.sharding import PartitionSpec as P

MESH = pl.DeviceIdType.MESH
f32 = jnp.float32
bf16 = jnp.bfloat16
leakage = 0.1
LANES = 128
SHARE = 8


class Plan:
    def __init__(self, planes, ranks, rows, halves, blocks, factor):
        self.N = planes
        self.P = ranks
        self.R = rows // ranks
        self.H = rows
        self.C = SHARE * ranks
        self.X = halves
        self.B = blocks
        self.U = planes // (halves * blocks)
        self.M = self.U * self.X
        self.KW = 9 * self.C
        self.NJ = self.KW // LANES + 1
        self.KP = self.NJ * LANES
        self.T = -(-3 * self.NJ // self.M)
        self.factor = factor


def kernel(
    g, vol, up, wl, bias,
    act_o, ig_o, wg_o, bg_o,
    VS, VX, UX, WS, WG, XL, DX, DL, W1, W2, PRE, DB, ACT, ACR, IGS, IGR,
    GT, GS, GR, SB, Q1, Q2, FIN,
    v_s, v_r, u_s, u_r, w_s, w_r, p_s, p_r, d_s, d_r, a_s, a_r, i_s, i_r,
    g_s, g_r, q1_s, q1_r, q2_s, q2_r, q3_s, q3_r,
):
    N, Pn, R, C, M, B, U = g.N, g.P, g.R, g.C, g.M, g.B, g.U
    s = lax.axis_index("space")
    r = lax.axis_index("chan")
    span = B * U
    x_lo, within = s // span, s % span
    block, unit = within // U, within % U
    member = x_lo * U + unit
    pending = []

    def chan_peer(k):
        return lax.rem(r + k, Pn)

    def group_peer(k):
        m = lax.rem(member + k, M)
        return m, (m // U) * span + block * U + m % U

    def block_peer(k):
        b = lax.rem(block + k, B)
        return x_lo * span + b * U + unit

    def copy(src, dst, ssem, rsem, to_s, to_r):
        return pltpu.make_async_remote_copy(
            src_ref=src, dst_ref=dst, send_sem=ssem, recv_sem=rsem,
            device_id=(to_s, to_r), device_id_type=MESH,
        )

    def start(c):
        c.start()
        pending.append((None, c))

    around = [(ds, dr) for ds in (-1, 0, 1) for dr in (-1, 0, 1) if (ds, dr) != (0, 0)]

    def inside(ds, dr):
        ok = None
        for here, step, end in ((s, ds, N), (r, dr, Pn)):
            if step:
                near = here > 0 if step < 0 else here < end - 1
                ok = near if ok is None else jnp.logical_and(ok, near)
        return ok

    barrier = pltpu.get_barrier_semaphore()

    def greet(to_s, to_r):
        pl.semaphore_signal(barrier, inc=1, device_id=(to_s, to_r), device_id_type=MESH)

    for k in range(1, Pn):
        greet(s, chan_peer(k))
    for k in range(1, M):
        greet(group_peer(k)[1], r)
    for k in range(1, B):
        greet(block_peer(k), r)
    for ds, dr in around:
        pl.when(inside(ds, dr))(functools.partial(greet, s + ds, r + dr))
    wide_s = 1 + jnp.where(s > 0, 1, 0) + jnp.where(s < N - 1, 1, 0)
    wide_r = 1 + jnp.where(r > 0, 1, 0) + jnp.where(r < Pn - 1, 1, 0)

    tile = (SHARE, LANES)
    zero_tile = jnp.zeros(tile, bf16)
    VS[0] = zero_tile
    VS[g.H + 1] = zero_tile
    VS[pl.ds(1, g.H)] = vol[...]
    lane8 = lax.broadcasted_iota(jnp.int32, tile, 1)
    edge = g.KW % LANES
    last = pl.ds((g.NJ - 1) * LANES, LANES)
    WS[...] = wl[...]
    b0 = bias[...]
    hi = b0.astype(bf16).astype(f32)
    mid = (b0 - hi).astype(bf16).astype(f32)
    low = (b0 - hi - mid).astype(bf16).astype(f32)
    tail = wl[0, :, last].astype(f32)
    tail = jnp.where(lane8 == edge, hi, tail)
    tail = jnp.where(lane8 == edge + 1, mid, tail)
    tail = jnp.where(lane8 == edge + 2, low, tail)
    WS[0, :, last] = tail.astype(bf16)

    pl.semaphore_wait(barrier, (Pn - 1) + (M - 1) + (B - 1) + wide_s * wide_r - 1)

    vsend, wsend, usend = [], [], []
    for k in range(1, Pn):
        to = chan_peer(k)
        c = copy(VS.at[pl.ds(R * to, R + 2)], VX.at[1, :, r], v_s.at[k], v_r.at[k], s, to)
        start(c)
        vsend.append(c)
    for k in range(1, Pn):
        c = copy(WS, WG.at[r], w_s.at[k], w_r.at[k], s, chan_peer(k))
        start(c)
        wsend.append(c)
    for k in range(1, Pn):
        to = chan_peer(k)
        c = copy(up.at[pl.ds(R * to, R)], UX.at[r], u_s.at[k], u_r.at[k], s, to)
        start(c)
        usend.append(c)
    VX[1, :, r] = VS[pl.ds(R * r, R + 2)]
    UX[r] = up[pl.ds(R * r, R)]
    WG[r] = WS[...]

    def clear(ref, a):
        def body(i, _):
            ref[a, i] = jnp.zeros(ref.shape[2:], bf16)
            return 0
        lax.fori_loop(0, R + 2, body, 0)

    @pl.when(s == 0)
    def _():
        clear(VX, 0)
        clear(DX, 0)

    @pl.when(s == N - 1)
    def _():
        clear(VX, 2)
        clear(DX, 2)

    @pl.when(r == 0)
    def _():
        for a in range(3):
            DX[a, 0] = jnp.zeros((C, LANES), bf16)

    @pl.when(r == Pn - 1)
    def _():
        for a in range(3):
            DX[a, R + 1] = jnp.zeros((C, LANES), bf16)

    for c in vsend:
        c.wait_recv()

    down = copy(VX.at[1], VX.at[2], p_s.at[0], p_r.at[0], s - 1, r)
    upw = copy(VX.at[1], VX.at[0], p_s.at[1], p_r.at[1], s + 1, r)
    pl.when(s > 0)(down.start)
    pl.when(s < N - 1)(upw.start)
    pending.append((s > 0, down))
    pending.append((s < N - 1, upw))

    lane = lax.broadcasted_iota(jnp.int32, (C, LANES), 1)

    def spread(ref, out, a):
        def body(i, _):
            x = ref[a, i].astype(f32).reshape(C, LANES)
            at = pl.ds(pl.multiple_of(i * LANES, LANES), LANES)
            before = jnp.where(lane == 0, 0.0, pltpu.roll(x, 1, 1))
            after = jnp.where(lane == LANES - 1, 0.0, pltpu.roll(x, LANES - 1, 1))
            out[pl.ds((3 * a) * C, C), at] = before.astype(bf16)
            out[pl.ds((3 * a + 1) * C, C), at] = x.astype(bf16)
            out[pl.ds((3 * a + 2) * C, C), at] = after.astype(bf16)
            return 0
        lax.fori_loop(0, R + 2, body, 0)

    spread(VX, XL, 1)

    for c in wsend:
        c.wait_recv()
    for b in range(3):
        whole = WG[:, b].astype(f32).reshape(C, g.KP)
        W1[b] = whole[:, : g.KW].astype(bf16)
        if b == 0:
            end = whole[:, g.KP - LANES :]
            own = jnp.logical_and(lane >= edge, lane < edge + 3)
            bcol = jnp.sum(jnp.where(own, end, 0.0), axis=1, keepdims=True)

    pl.when(s < N - 1)(down.wait_recv)
    pl.when(s > 0)(upw.wait_recv)
    spread(VX, XL, 0)
    spread(VX, XL, 2)

    def conv(w, x):
        acc = None
        for b in range(3):
            part = jnp.dot(w[b], x[:, pl.ds(b * LANES, R * LANES)], preferred_element_type=f32)
            acc = part if acc is None else acc + part
        return acc

    PRE[...] = conv(W1, XL)

    for c in usend:
        c.wait_recv()

    dsum = jnp.zeros((C, LANES), f32)
    for j in range(R):
        p = PRE[:, pl.ds(j * LANES, LANES)] + bcol
        e = jnp.exp(-jnp.abs(p))
        soft = jnp.maximum(p, 0.0) + jnp.log(1.0 + e)
        gate = jnp.where(p >= 0.0, 1.0, e) / (1.0 + e)
        act = leakage * p + (1.0 - leakage) * soft
        ACT[:, j] = act.reshape(Pn, SHARE, LANES).astype(bf16)
        u = UX[:, j].astype(f32).reshape(C, LANES)
        d = (u * (leakage + (1.0 - leakage) * gate)).astype(bf16)
        DX[1, 1 + j] = d
        DB[:, pl.ds(j * LANES, LANES)] = d
        dsum = dsum + d.astype(f32)

    dcopies = []
    for e, (ds, dr) in enumerate(around):
        if dr == 0:
            src, dst = DX.at[1, pl.ds(1, R)], DX.at[1 - ds, pl.ds(1, R)]
        elif dr < 0:
            src, dst = DX.at[1, 1], DX.at[1 - ds, R + 1]
        else:
            src, dst = DX.at[1, R], DX.at[1 - ds, 0]
        c = copy(src, dst, d_s.at[e], d_r.at[e], s + ds, r + dr)
        pl.when(inside(ds, dr))(c.start)
        pending.append((inside(ds, dr), c))
        dcopies.append((inside(-ds, -dr), c))

    asend = []
    for k in range(1, Pn):
        to = chan_peer(k)
        c = copy(ACT.at[to], ACR.at[r], a_s.at[k], a_r.at[k], s, to)
        start(c)
        asend.append(c)
    ACR[r] = ACT[r]

    dcol = jnp.sum(dsum, axis=1, keepdims=True)
    for b in range(3):
        GT[b, :, pl.ds(0, g.KW)] = lax.dot_general(
            DB[...], XL[:, pl.ds(b * LANES, R * LANES)],
            (((1,), (1,)), ((), ())), preferred_element_type=f32,
        )
        cur = GT[b, :, last]
        cur = jnp.where(lane < edge, cur, 0.0)
        if b == 0:
            cur = jnp.where(lane == edge, dcol, cur)
        GT[b, :, last] = cur
        for to in range(Pn):
            GS[to, b] = GT[b, pl.ds(SHARE * to, SHARE), :].astype(GS.dtype)
    gsend = []
    for k in range(1, Pn):
        to = chan_peer(k)
        c = copy(GS.at[to], GR.at[r], g_s.at[k], g_r.at[k], s, to)
        start(c)
        gsend.append(c)
    GR[r] = GS[r]

    for b in range(3):
        whole = W1[2 - b].astype(f32).T
        blocks = []
        for a in range(3):
            for c_ in range(3):
                at = ((2 - a) * 3 + (2 - c_)) * C
                blocks.append(whole[at : at + C])
        W2[b] = jnp.concatenate(blocks, axis=1).astype(bf16)

    for ok, c in dcopies:
        pl.when(ok)(c.wait_recv)
    for a in range(3):
        spread(DX, DL, a)
    PRE[...] = conv(W2, DL)
    for j in range(R):
        v = PRE[:, pl.ds(j * LANES, LANES)]
        IGS[:, j] = v.reshape(Pn, SHARE, LANES).astype(bf16)
    isend = []
    for k in range(1, Pn):
        to = chan_peer(k)
        c = copy(IGS.at[to], IGR.at[r], i_s.at[k], i_r.at[k], s, to)
        start(c)
        isend.append(c)
    IGR[r] = IGS[r]

    for c in gsend:
        c.wait_recv()
    for b in range(3):
        acc = GR[0, b].astype(f32)
        for q in range(1, Pn):
            acc = acc + GR[q, b].astype(f32)
        for j in range(g.NJ):
            t = b * g.NJ + j
            SB[t // g.T, t % g.T] = acc[:, j * LANES : (j + 1) * LANES]
    for t in range(3 * g.NJ, M * g.T):
        SB[t // g.T, t % g.T] = jnp.zeros(tile, f32)
    q1send = []
    for k in range(1, M):
        m, to_s = group_peer(k)
        c = copy(SB.at[m], Q1.at[member], q1_s.at[k], q1_r.at[k], to_s, r)
        start(c)
        q1send.append(c)
    Q1[member] = SB[member]

    for c in asend:
        c.wait_recv()
    act_o[...] = ACR[...]

    for c in q1send:
        c.wait_recv()
    acc = Q1[0]
    for m in range(1, M):
        acc = acc + Q1[m]
    Q2[block] = acc
    q2send = []
    for k in range(1, B):
        c = copy(Q2.at[block], Q2.at[block], q2_s.at[k], q2_r.at[k], block_peer(k), r)
        start(c)
        q2send.append(c)
    for c in isend:
        c.wait_recv()
    ig_o[...] = IGR[...]
    for c in q2send:
        c.wait_recv()
    acc = Q2[0]
    for m in range(1, B):
        acc = acc + Q2[m]
    FIN[member] = acc * g.factor
    q3send = []
    for k in range(1, M):
        c = copy(FIN.at[member], FIN.at[member], q3_s.at[k], q3_r.at[k], group_peer(k)[1], r)
        start(c)
        q3send.append(c)
    for c in q3send:
        c.wait_recv()
    for a in range(3):
        for b in range(3):
            for c_ in range(3):
                at = (a * 3 + c_) * C
                t = b * g.NJ + at // LANES
                off = at % LANES
                wg_o[(a * 3 + b) * 3 + c_] = FIN[t // g.T, t % g.T][:, off : off + C]
    t = g.NJ - 1
    bg_o[...] = FIN[t // g.T, t % g.T]

    for ok, c in pending:
        if ok is None:
            c.wait_send()
        else:
            pl.when(ok)(c.wait_send)


def shards(g, volume, weight, bias, upstream):
    N, Pn, R, C, M, B = g.N, g.P, g.R, g.C, g.M, g.B
    vol = jnp.transpose(volume[:, 0], (1, 0, 2))
    up = jnp.transpose(upstream[:, 0], (1, 0, 2))
    wl = jnp.transpose(weight, (3, 0, 2, 4, 1)).reshape(3, SHARE, g.KW)
    wl = jnp.pad(wl, ((0, 0), (0, 0), (0, g.KP - g.KW)))
    bt = jnp.broadcast_to(bias[:, None], (SHARE, LANES))
    sds = jax.ShapeDtypeStruct
    vm = pl.BlockSpec(memory_space=pltpu.VMEM)
    rows = (R + 2) * LANES
    dma = pltpu.SemaphoreType.DMA
    V = pltpu.VMEM
    chan = [dma((Pn,)), dma((Pn,))]
    scratch = [
        V((g.H + 2, SHARE, LANES), bf16),
        V((3, R + 2, Pn, SHARE, LANES), bf16),
        V((Pn, R, SHARE, LANES), bf16),
        V((3, SHARE, g.KP), bf16),
        V((Pn, 3, SHARE, g.KP), bf16),
        V((9 * C, rows), bf16),
        V((3, R + 2, C, LANES), bf16),
        V((9 * C, rows), bf16),
        V((3, C, g.KW), bf16),
        V((3, C, g.KW), bf16),
        V((C, R * LANES), f32),
        V((C, R * LANES), bf16),
        V((Pn, R, SHARE, LANES), bf16),
        V((Pn, R, SHARE, LANES), bf16),
        V((Pn, R, SHARE, LANES), bf16),
        V((Pn, R, SHARE, LANES), bf16),
        V((3, C, g.KP), f32),
        V((Pn, 3, SHARE, g.KP), bf16),
        V((Pn, 3, SHARE, g.KP), bf16),
        V((M, g.T, SHARE, LANES), f32),
        V((M, g.T, SHARE, LANES), f32),
        V((B, g.T, SHARE, LANES), f32),
        V((M, g.T, SHARE, LANES), f32),
        *chan, *chan, *chan,
        dma((2,)), dma((2,)),
        dma((8,)), dma((8,)),
        *chan, *chan, *chan,
        dma((M,)), dma((M,)),
        dma((B,)), dma((B,)),
        dma((M,)), dma((M,)),
    ]
    act, ig, wg, bg = pl.pallas_call(
        functools.partial(kernel, g),
        out_shape=(
            sds((Pn, R, SHARE, LANES), bf16),
            sds((Pn, R, SHARE, LANES), bf16),
            sds((27, SHARE, C), f32),
            sds((SHARE, LANES), f32),
        ),
        in_specs=[vm] * 4,
        out_specs=(vm,) * 4,
        scratch_shapes=scratch,
        compiler_params=pltpu.CompilerParams(
            collective_id=0, has_side_effects=True, vmem_limit_bytes=40 << 20
        ),
    )(vol, up, wl, bt)

    def back(x):
        return jnp.transpose(x.reshape(g.H, SHARE, LANES), (1, 0, 2))[:, None]

    wgrad = jnp.transpose(wg.reshape(3, 3, 3, SHARE, C), (3, 4, 0, 1, 2))
    return back(act), back(ig), wgrad, bg[:, g.KW % LANES]


def solution(mesh, rows=48, halves=2, blocks=4):
    planes, ranks = mesh.shape["space"], mesh.shape["chan"]
    factor = 1.0 / math.sqrt(planes * rows * LANES)
    g = Plan(planes, ranks, rows, halves, blocks, factor)
    field = P("chan", "space", None, None)
    filters = P("chan", None, None, None, None)
    return jax.shard_map(
        functools.partial(shards, g),
        mesh=mesh,
        in_specs=(field, filters, P("chan"), field),
        out_specs=(field, field, filters, P("chan")),
        check_vma=False,
    )
```

time: 500 us -> 59 us (0.12)
  blocking collectives: 320 us -> 0 us
  matrix products: 88.7 us -> 0 us
  Pallas kernels: 0 us -> 52.9 us
  local copies, waits for them, and re-layouts: 49.2 us -> 5.18 us
  starting transfers between devices: 23.4 us -> 0 us
  other arithmetic: 12.4 us -> 0 us
    psum x1 -> x0, blocking collectives: 205 us -> none  [shards(): summed_w, summed_b = lax.psum((partial_w, partial_b), 'space')]
    all_gather x3 -> x0, blocking collectives: 115 us -> none  [the longest x1 42.9 us: shards(): delta_all = lax.all_gather(delta, 'chan', axis=0, tiled=True)]
    transpose x1 -> x0, matrix products: 67 us -> none  [shards(): partial_w = jnp.transpose(partial_w, (1, 0, 2, 3, 4))]
    pallas_call x0 -> x1, Pallas kernels: none -> 52.9 us  [shards(): pl.pallas_call(functools.partial(kernel, g), out_shape=(sds((Pn, R, SHARE...]
    ppermute x4 -> x0, starting transfers between devices: 23.4 us -> none  [the longest x2 19.5 us: padded(): after = lax.ppermute(first, axis, down)]
    conv_general_dilated x2 -> x0, matrix products: 21.7 us -> none  [convolve(): lax.conv_general_dilated(lhs, rhs, (1, 1, 1), padding, dimension_numbers=...]
    conv_general_dilated x6 -> x0, local copies, waits for them, and re-layouts: 16.2 us -> none  [convolve(): lax.conv_general_dilated(lhs, rhs, (1, 1, 1), padding, dimension_numbers=...]
    ppermute x4 -> x0, local copies, waits for them, and re-layouts: 14.7 us -> none  [the longest x2 7.75 us: padded(): before = lax.ppermute(last, axis, up)]
  transfers between devices with their start and end apart: 4 -> 0, of which waited for: 0 -> 0; matrix products, arithmetic and copies ran while one was open for 17% -> 0% of each run, Pallas kernels for 0% -> 0%
where the time goes in v1:
time: 59 us; the launch traced here: 58.8 us
  Pallas kernels  52.9 us (90%)
  local copies, waits for them, and re-layouts  5.18 us (9%)
  between operations  0.68 us (1%)
    pallas_call x1, Pallas kernels, shards(): pl.pallas_call(functools.partial(kernel, g), out_shape=(sds((Pn, R, SHARE...  52.9 us
    unnamed x7, local copies, waits for them, and re-layouts  2.05 us
    reshape x2, local copies, waits for them, and re-layouts, back(): return jnp.transpose(x.reshape(g.H, SHARE, LANES), (1, 0, 2))[:, None]  1.31 us

profile of v1, /device:TPU:1, one launch (start us, length us, event | category | flops | bytes accessed | tf_op | source)
XLA Modules:
  0.0 58.8 jit_solution(9637784536819988831)
XLA Ops:
  0.6 0.0 copy-start.2
  0.6 0.6 %copy-done.2 = f32[8]{0:T(128)S(1)} copy-done((f32[8]{0:T(128)S(1)}, f32[8]{0:T(128)}, u32[]{:S(2)}) %copy-start.2) | copy-done | bytes 56
  1.3 0.1 broadcast_in_dim.12.bias
  1.4 0.0 copy-start.1
  1.4 0.9 %copy.15 = bf16[3,8,3,3,64]{4,3,2,1,0:T(4,128)(2,1)S(1)} copy(bf16[3,8,3,3,64]{4,1,3,0,2:T(8,128)(2,1)} %bitcast.29) | data formatting | bytes 55296 | tf_op jit(solution)/shard_map/transpose | solution.py:372
  2.2 0.0 copy-start
  2.2 0.1 reshape.21
  2.4 0.0 copy-done.1
  2.4 0.7 %copy-done = bf16[8,1,48,128]{3,2,1,0:T(8,128)(2,1)S(1)} copy-done((bf16[8,1,48,128]{3,2,1,0:T(8,128)(2,1)S(1)}, bf16[8,1,48,128]{3,2,1,0:T(8,128)(2,1)}, u32[]{:S(2)}) %copy-start) | copy-done | bytes 98328
  3.1 0.1 copy_bitcast_fusion.2
  3.2 52.9 %shard_map.75 = (bf16[8,6,8,128]{3,2,1,0:T(8,128)(2,1)S(1)}, bf16[8,6,8,128]{3,2,1,0:T(8,128)(2,1)S(1)}, f32[27,8,64]{2,1,0:T(8,128)S(1)}, f32[8,128]{1,0:T(8,128)S(1)}) custom-call(bf16[48,8,128]{2,1,0:T(8,128)(2,1)S(1)} %get-tuple-element.13.vol, bf16[48,8,128]{2,1,0:T(8,128)(2,1)S(1)} %get-tuple-element.12.up, bf16[3,8,640]{2,1,0:T(8,128)(2,1)S(1)} %pad.4.wl, ...), custom_call_target="tpu_custom_call" | custom-call | tf_op jit(solution)/shard_map/pallas_call | solution.py:413
  56.1 0.7 %copy.23 = bf16[48,8,128]{2,0,1:T(8,128)(2,1)} copy(bf16[48,8,128]{2,1,0:T(8,128)(2,1)S(1)} %bitcast.26) | data formatting | bytes 196608 | tf_op jit(solution)/shard_map/reshape | solution.py:430
  56.8 0.7 %copy.22 = bf16[48,8,128]{2,0,1:T(8,128)(2,1)} copy(bf16[48,8,128]{2,1,0:T(8,128)(2,1)S(1)} %bitcast.25) | data formatting | bytes 196608 | tf_op jit(solution)/shard_map/reshape | solution.py:430
  57.5 0.7 %slice_reduce_fusion = f32[8]{0:T(128)} fusion(f32[8,128]{1,0:T(8,128)S(1)} %get-tuple-element.11), kind=kLoop, calls=%fused_computation.4 | loop fusion | bytes 64 | tf_op jit(solution)/shard_map/slice | solution.py:433
  58.2 0.6 %copy.25 = f32[8,64,3,3,3]{1,0,4,3,2:T(8,128)} copy(f32[8,64,3,3,3]{1,0,4,3,2:T(8,128)S(1)} %bitcast.24) | data formatting | bytes 110592
  (1 shorter events, 0.0 us)
Async XLA Ops:
  0.6 0.7 %copy-start.2 = (f32[8]{0:T(128)S(1)}, f32[8]{0:T(128)}, u32[]{:S(2)}) copy-start(f32[8]{0:T(128)} %param.6) | copy-start | bytes 100
  1.4 1.0 %copy-start.1 = (bf16[8,1,48,128]{3,2,1,0:T(8,128)(2,1)S(1)}, bf16[8,1,48,128]{3,2,1,0:T(8,128)(2,1)}, u32[]{:S(2)}) copy-start(bf16[8,1,48,128]{3,2,1,0:T(8,128)(2,1)} %param.4) | copy-start | bytes 294916
  2.2 0.9 %copy-start = (bf16[8,1,48,128]{3,2,1,0:T(8,128)(2,1)S(1)}, bf16[8,1,48,128]{3,2,1,0:T(8,128)(2,1)}, u32[]{:S(2)}) copy-start(bf16[8,1,48,128]{3,2,1,0:T(8,128)(2,1)} %param.7) | copy-start | bytes 294916

commit v2 on v1

--- a/solution.py
+++ b/solution.py
@@ -37,9 +37,9 @@
 def kernel(
     g, vol, up, wl, bias,
     act_o, ig_o, wg_o, bg_o,
-    VS, VX, UX, WS, WG, XL, DX, DL, W1, W2, PRE, DB, ACT, ACR, IGS, IGR,
-    GT, GS, GR, SB, Q1, Q2, FIN,
-    v_s, v_r, u_s, u_r, w_s, w_r, p_s, p_r, d_s, d_r, a_s, a_r, i_s, i_r,
+    RAW, RAWW, TALL, SEND, RCV, HV, XL, DX, DL, W1, W2, PRE, DB, AIS, AIR,
+    GT, GS, GR, SB, Q1, Q2, FIN, OUTS, OUTW, OUTB,
+    l_s, o_s, v_s, v_r, p_s, p_r, d_s, d_r, i_s, i_r,
     g_s, g_r, q1_s, q1_r, q2_s, q2_r, q3_s, q3_r,
 ):
     N, Pn, R, C, M, B, U = g.N, g.P, g.R, g.C, g.M, g.B, g.U
@@ -98,45 +98,55 @@
     wide_s = 1 + jnp.where(s > 0, 1, 0) + jnp.where(s < N - 1, 1, 0)
     wide_r = 1 + jnp.where(r > 0, 1, 0) + jnp.where(r < Pn - 1, 1, 0)
 
+    V, Wt = R + 2, 2 * R + 2
+    loads = [
+        pltpu.make_async_copy(vol, RAW.at[0], l_s.at[0]),
+        pltpu.make_async_copy(up, RAW.at[1], l_s.at[1]),
+        pltpu.make_async_copy(wl, RAWW, l_s.at[2]),
+    ]
+    for c in loads:
+        c.start()
     tile = (SHARE, LANES)
-    zero_tile = jnp.zeros(tile, bf16)
-    VS[0] = zero_tile
-    VS[g.H + 1] = zero_tile
-    VS[pl.ds(1, g.H)] = vol[...]
-    lane8 = lax.broadcasted_iota(jnp.int32, tile, 1)
     edge = g.KW % LANES
-    last = pl.ds((g.NJ - 1) * LANES, LANES)
-    WS[...] = wl[...]
-    b0 = bias[...]
+    for c in loads:
+        c.wait()
+    sub = lax.broadcasted_iota(jnp.int32, (SHARE, g.KP - g.KW), 0)
+    col = lax.broadcasted_iota(jnp.int32, (SHARE, g.KP - g.KW), 1)
+    b0 = jnp.zeros((SHARE, g.KP - g.KW), f32)
+    for q in range(SHARE):
+        b0 = jnp.where(sub == q, bias[q], b0)
     hi = b0.astype(bf16).astype(f32)
     mid = (b0 - hi).astype(bf16).astype(f32)
     low = (b0 - hi - mid).astype(bf16).astype(f32)
-    tail = wl[0, :, last].astype(f32)
-    tail = jnp.where(lane8 == edge, hi, tail)
-    tail = jnp.where(lane8 == edge + 1, mid, tail)
-    tail = jnp.where(lane8 == edge + 2, low, tail)
-    WS[0, :, last] = tail.astype(bf16)
+    tail = jnp.where(col == 0, hi, jnp.where(col == 1, mid, jnp.where(col == 2, low, 0.0)))
+    for b in range(3):
+        taps = [RAWW[(a * 3 + b) * 3 + c_].astype(f32) for a in range(3) for c_ in range(3)]
+        whole = jnp.concatenate(taps + [tail], axis=1)
+        for j in range(g.NJ):
+            part = whole[:, j * LANES : (j + 1) * LANES].astype(bf16)
+            for to in range(Pn):
+                SEND[to, Wt + b * g.NJ + j] = part
+    for n in range(2):
+        TALL[n] = RAW[n].astype(f32).reshape(SHARE * g.H, LANES)
+    zero_tile = jnp.zeros(tile, bf16)
+    SEND[0, 0] = zero_tile
+    SEND[Pn - 1, R + 1] = zero_tile
+    for h in range(g.H):
+        row = TALL[0, pl.ds(h, SHARE, stride=g.H), :].astype(bf16)
+        for to in range(Pn):
+            if 0 <= h + 1 - R * to < V:
+                SEND[to, h + 1 - R * to] = row
+        SEND[h // R, V + h % R] = TALL[1, pl.ds(h, SHARE, stride=g.H), :].astype(bf16)
 
     pl.semaphore_wait(barrier, (Pn - 1) + (M - 1) + (B - 1) + wide_s * wide_r - 1)
 
-    vsend, wsend, usend = [], [], []
+    vsend = []
     for k in range(1, Pn):
         to = chan_peer(k)
-        c = copy(VS.at[pl.ds(R * to, R + 2)], VX.at[1, :, r], v_s.at[k], v_r.at[k], s, to)
+        c = copy(SEND.at[to], RCV.at[r], v_s.at[k], v_r.at[k], s, to)
         start(c)
         vsend.append(c)
-    for k in range(1, Pn):
-        c = copy(WS, WG.at[r], w_s.at[k], w_r.at[k], s, chan_peer(k))
-        start(c)
-        wsend.append(c)
-    for k in range(1, Pn):
-        to = chan_peer(k)
-        c = copy(up.at[pl.ds(R * to, R)], UX.at[r], u_s.at[k], u_r.at[k], s, to)
-        start(c)
-        usend.append(c)
-    VX[1, :, r] = VS[pl.ds(R * r, R + 2)]
-    UX[r] = up[pl.ds(R * r, R)]
-    WG[r] = WS[...]
+    RCV[r] = SEND[r]
 
     def clear(ref, a):
         def body(i, _):
@@ -144,14 +154,20 @@
             return 0
         lax.fori_loop(0, R + 2, body, 0)
 
+    def clear_rows(ref, a):
+        def body(i, _):
+            ref[a, i] = jnp.zeros(ref.shape[2:], bf16)
+            return 0
+        lax.fori_loop(0, Pn, body, 0)
+
     @pl.when(s == 0)
     def _():
-        clear(VX, 0)
+        clear_rows(HV, 0)
         clear(DX, 0)
 
     @pl.when(s == N - 1)
     def _():
-        clear(VX, 2)
+        clear_rows(HV, 1)
         clear(DX, 2)
 
     @pl.when(r == 0)
@@ -167,18 +183,20 @@
     for c in vsend:
         c.wait_recv()
 
-    down = copy(VX.at[1], VX.at[2], p_s.at[0], p_r.at[0], s - 1, r)
-    upw = copy(VX.at[1], VX.at[0], p_s.at[1], p_r.at[1], s + 1, r)
+    mine = RCV.at[:, pl.ds(0, V)]
+    down = copy(mine, HV.at[1], p_s.at[0], p_r.at[0], s - 1, r)
+    upw = copy(mine, HV.at[0], p_s.at[1], p_r.at[1], s + 1, r)
     pl.when(s > 0)(down.start)
     pl.when(s < N - 1)(upw.start)
     pending.append((s > 0, down))
     pending.append((s < N - 1, upw))
 
+    last = pl.ds((g.NJ - 1) * LANES, LANES)
     lane = lax.broadcasted_iota(jnp.int32, (C, LANES), 1)
 
-    def spread(ref, out, a):
+    def spread(row, out, a):
         def body(i, _):
-            x = ref[a, i].astype(f32).reshape(C, LANES)
+            x = row(i).astype(f32).reshape(C, LANES)
             at = pl.ds(pl.multiple_of(i * LANES, LANES), LANES)
             before = jnp.where(lane == 0, 0.0, pltpu.roll(x, 1, 1))
             after = jnp.where(lane == LANES - 1, 0.0, pltpu.roll(x, LANES - 1, 1))
@@ -188,12 +206,12 @@
             return 0
         lax.fori_loop(0, R + 2, body, 0)
 
-    spread(VX, XL, 1)
-
-    for c in wsend:
-        c.wait_recv()
+    spread(lambda i: RCV[:, i], XL, 1)
+
     for b in range(3):
-        whole = WG[:, b].astype(f32).reshape(C, g.KP)
+        whole = jnp.concatenate(
+            [RCV[:, Wt + b * g.NJ + j].astype(f32).reshape(C, LANES) for j in range(g.NJ)], axis=1
+        )
         W1[b] = whole[:, : g.KW].astype(bf16)
         if b == 0:
             end = whole[:, g.KP - LANES :]
@@ -202,8 +220,8 @@
 
     pl.when(s < N - 1)(down.wait_recv)
     pl.when(s > 0)(upw.wait_recv)
-    spread(VX, XL, 0)
-    spread(VX, XL, 2)
+    spread(lambda i: HV[0, :, i], XL, 0)
+    spread(lambda i: HV[1, :, i], XL, 2)
 
     def conv(w, x):
         acc = None
@@ -213,9 +231,6 @@
         return acc
 
     PRE[...] = conv(W1, XL)
-
-    for c in usend:
-        c.wait_recv()
 
     dsum = jnp.zeros((C, LANES), f32)
     for j in range(R):
@@ -224,33 +239,12 @@
         soft = jnp.maximum(p, 0.0) + jnp.log(1.0 + e)
         gate = jnp.where(p >= 0.0, 1.0, e) / (1.0 + e)
         act = leakage * p + (1.0 - leakage) * soft
-        ACT[:, j] = act.reshape(Pn, SHARE, LANES).astype(bf16)
-        u = UX[:, j].astype(f32).reshape(C, LANES)
+        AIS[:, 0, j] = act.reshape(Pn, SHARE, LANES).astype(bf16)
+        u = RCV[:, V + j].astype(f32).reshape(C, LANES)
         d = (u * (leakage + (1.0 - leakage) * gate)).astype(bf16)
         DX[1, 1 + j] = d
         DB[:, pl.ds(j * LANES, LANES)] = d
         dsum = dsum + d.astype(f32)
-
-    dcopies = []
-    for e, (ds, dr) in enumerate(around):
-        if dr == 0:
-            src, dst = DX.at[1, pl.ds(1, R)], DX.at[1 - ds, pl.ds(1, R)]
-        elif dr < 0:
-            src, dst = DX.at[1, 1], DX.at[1 - ds, R + 1]
-        else:
-            src, dst = DX.at[1, R], DX.at[1 - ds, 0]
-        c = copy(src, dst, d_s.at[e], d_r.at[e], s + ds, r + dr)
-        pl.when(inside(ds, dr))(c.start)
-        pending.append((inside(ds, dr), c))
-        dcopies.append((inside(-ds, -dr), c))
-
-    asend = []
-    for k in range(1, Pn):
-        to = chan_peer(k)
-        c = copy(ACT.at[to], ACR.at[r], a_s.at[k], a_r.at[k], s, to)
-        start(c)
-        asend.append(c)
-    ACR[r] = ACT[r]
 
     dcol = jnp.sum(dsum, axis=1, keepdims=True)
     for b in range(3):
@@ -273,6 +267,19 @@
         gsend.append(c)
     GR[r] = GS[r]
 
+    dcopies = []
+    for e, (ds, dr) in enumerate(around):
+        if dr == 0:
+            src, dst = DX.at[1, pl.ds(1, R)], DX.at[1 - ds, pl.ds(1, R)]
+        elif dr < 0:
+            src, dst = DX.at[1, 1], DX.at[1 - ds, R + 1]
+        else:
+            src, dst = DX.at[1, R], DX.at[1 - ds, 0]
+        c = copy(src, dst, d_s.at[e], d_r.at[e], s + ds, r + dr)
+        pl.when(inside(ds, dr))(c.start)
+        pending.append((inside(ds, dr), c))
+        dcopies.append((inside(-ds, -dr), c))
+
     for b in range(3):
         whole = W1[2 - b].astype(f32).T
         blocks = []
@@ -281,22 +288,6 @@
                 at = ((2 - a) * 3 + (2 - c_)) * C
                 blocks.append(whole[at : at + C])
         W2[b] = jnp.concatenate(blocks, axis=1).astype(bf16)
-
-    for ok, c in dcopies:
-        pl.when(ok)(c.wait_recv)
-    for a in range(3):
-        spread(DX, DL, a)
-    PRE[...] = conv(W2, DL)
-    for j in range(R):
-        v = PRE[:, pl.ds(j * LANES, LANES)]
-        IGS[:, j] = v.reshape(Pn, SHARE, LANES).astype(bf16)
-    isend = []
-    for k in range(1, Pn):
-        to = chan_peer(k)
-        c = copy(IGS.at[to], IGR.at[r], i_s.at[k], i_r.at[k], s, to)
-        start(c)
-        isend.append(c)
-    IGR[r] = IGS[r]
 
     for c in gsend:
         c.wait_recv()
@@ -317,9 +308,21 @@
         q1send.append(c)
     Q1[member] = SB[member]
 
-    for c in asend:
-        c.wait_recv()
-    act_o[...] = ACR[...]
+    for ok, c in dcopies:
+        pl.when(ok)(c.wait_recv)
+    for a in range(3):
+        spread(lambda i, a=a: DX[a, i], DL, a)
+    PRE[...] = conv(W2, DL)
+    for j in range(R):
+        v = PRE[:, pl.ds(j * LANES, LANES)]
+        AIS[:, 1, j] = v.reshape(Pn, SHARE, LANES).astype(bf16)
+    isend = []
+    for k in range(1, Pn):
+        to = chan_peer(k)
+        c = copy(AIS.at[to], AIR.at[r], i_s.at[k], i_r.at[k], s, to)
+        start(c)
+        isend.append(c)
+    AIR[r] = AIS[r]
 
     for c in q1send:
         c.wait_recv()
@@ -334,7 +337,13 @@
         q2send.append(c)
     for c in isend:
         c.wait_recv()
-    ig_o[...] = IGR[...]
+    leave = []
+    for n, out in enumerate((act_o, ig_o)):
+        TALL[n] = AIR[:, n].astype(f32).reshape(g.H * SHARE, LANES)
+        for q in range(SHARE):
+            OUTS[n, q] = TALL[n, pl.ds(q, g.H, stride=SHARE), :].astype(bf16)
+        leave.append(pltpu.make_async_copy(OUTS.at[n], out, o_s.at[n]))
+        leave[n].start()
     for c in q2send:
         c.wait_recv()
     acc = Q2[0]
@@ -354,36 +363,50 @@
                 at = (a * 3 + c_) * C
                 t = b * g.NJ + at // LANES
                 off = at % LANES
-                wg_o[(a * 3 + b) * 3 + c_] = FIN[t // g.T, t % g.T][:, off : off + C]
+                OUTW[(a * 3 + b) * 3 + c_] = FIN[t // g.T, t % g.T][:, off : off + C]
     t = g.NJ - 1
-    bg_o[...] = FIN[t // g.T, t % g.T]
+    sums = FIN[t // g.T, t % g.T][:, edge : edge + 1]
+    spot = lax.broadcasted_iota(jnp.int32, tile, 0) == lax.broadcasted_iota(jnp.int32, tile, 1)
+    OUTB[...] = jnp.sum(jnp.where(spot, sums, 0.0), axis=0, keepdims=True)[:, :SHARE]
+    for n, (a, b) in enumerate(((OUTW, wg_o), (OUTB, bg_o))):
+        leave.append(pltpu.make_async_copy(a, b, o_s.at[2 + n]))
+        leave[-1].start()
 
     for ok, c in pending:
         if ok is None:
             c.wait_send()
         else:
             pl.when(ok)(c.wait_send)
+    for c in leave:
+        c.wait()
+
+
+def deliver(act, ig, wg, bg, act_o, ig_o, wg_o, bg_o, sems):
+    pairs = ((act, act_o), (ig, ig_o), (wg, wg_o), (bg, bg_o))
+    moves = [pltpu.make_async_copy(a, b, sems.at[i]) for i, (a, b) in enumerate(pairs)]
+    for c in moves:
+        c.start()
+    for c in moves:
+        c.wait()
 
 
 def shards(g, volume, weight, bias, upstream):
-    N, Pn, R, C, M, B = g.N, g.P, g.R, g.C, g.M, g.B
-    vol = jnp.transpose(volume[:, 0], (1, 0, 2))
-    up = jnp.transpose(upstream[:, 0], (1, 0, 2))
-    wl = jnp.transpose(weight, (3, 0, 2, 4, 1)).reshape(3, SHARE, g.KW)
-    wl = jnp.pad(wl, ((0, 0), (0, 0), (0, g.KP - g.KW)))
-    bt = jnp.broadcast_to(bias[:, None], (SHARE, LANES))
+    Pn, R, C, M, B = g.P, g.R, g.C, g.M, g.B
+    vol, up = volume[:, 0], upstream[:, 0]
+    wl = jnp.transpose(weight, (2, 3, 4, 0, 1)).reshape(27, SHARE, C)
     sds = jax.ShapeDtypeStruct
-    vm = pl.BlockSpec(memory_space=pltpu.VMEM)
+    hbm = pl.BlockSpec(memory_space=pltpu.HBM)
     rows = (R + 2) * LANES
     dma = pltpu.SemaphoreType.DMA
     V = pltpu.VMEM
     chan = [dma((Pn,)), dma((Pn,))]
     scratch = [
-        V((g.H + 2, SHARE, LANES), bf16),
-        V((3, R + 2, Pn, SHARE, LANES), bf16),
-        V((Pn, R, SHARE, LANES), bf16),
-        V((3, SHARE, g.KP), bf16),
-        V((Pn, 3, SHARE, g.KP), bf16),
+        V((2, SHARE, g.H, LANES), bf16),
+        V((27, SHARE, C), bf16),
+        V((2, SHARE * g.H, LANES), f32),
+        V((Pn, 2 * R + 2 + 3 * g.NJ, SHARE, LANES), bf16),
+        V((Pn, 2 * R + 2 + 3 * g.NJ, SHARE, LANES), bf16),
+        V((2, Pn, R + 2, SHARE, LANES), bf16),
         V((9 * C, rows), bf16),
         V((3, R + 2, C, LANES), bf16),
         V((9 * C, rows), bf16),
@@ -391,10 +414,8 @@
         V((3, C, g.KW), bf16),
         V((C, R * LANES), f32),
         V((C, R * LANES), bf16),
-        V((Pn, R, SHARE, LANES), bf16),
-        V((Pn, R, SHARE, LANES), bf16),
-        V((Pn, R, SHARE, LANES), bf16),
-        V((Pn, R, SHARE, LANES), bf16),
+        V((Pn, 2, R, SHARE, LANES), bf16),
+        V((Pn, 2, R, SHARE, LANES), bf16),
         V((3, C, g.KP), f32),
         V((Pn, 3, SHARE, g.KP), bf16),
         V((Pn, 3, SHARE, g.KP), bf16),
@@ -402,10 +423,15 @@
         V((M, g.T, SHARE, LANES), f32),
         V((B, g.T, SHARE, LANES), f32),
         V((M, g.T, SHARE, LANES), f32),
-        *chan, *chan, *chan,
+        V((2, SHARE, g.H, LANES), bf16),
+        V((27, SHARE, C), f32),
+        V((1, SHARE), f32),
+        dma((3,)),
+        dma((4,)),
+        *chan,
         dma((2,)), dma((2,)),
         dma((8,)), dma((8,)),
-        *chan, *chan, *chan,
+        *chan, *chan,
         dma((M,)), dma((M,)),
         dma((B,)), dma((B,)),
         dma((M,)), dma((M,)),
@@ -413,27 +439,35 @@
     act, ig, wg, bg = pl.pallas_call(
         functools.partial(kernel, g),
         out_shape=(
-            sds((Pn, R, SHARE, LANES), bf16),
-            sds((Pn, R, SHARE, LANES), bf16),
+            sds((SHARE, g.H, LANES), bf16),
+            sds((SHARE, g.H, LANES), bf16),
             sds((27, SHARE, C), f32),
-            sds((SHARE, LANES), f32),
+            sds((1, SHARE), f32),
         ),
-        in_specs=[vm] * 4,
-        out_specs=(vm,) * 4,
+        in_specs=[hbm, hbm, hbm, pl.BlockSpec(memory_space=pltpu.SMEM)],
+        out_specs=(hbm,) * 4,
         scratch_shapes=scratch,
         compiler_params=pltpu.CompilerParams(
-            collective_id=0, has_side_effects=True, vmem_limit_bytes=40 << 20
+            collective_id=0, has_side_effects=True, vmem_limit_bytes=62 << 20
         ),
-    )(vol, up, wl, bt)
-
-    def back(x):
-        return jnp.transpose(x.reshape(g.H, SHARE, LANES), (1, 0, 2))[:, None]
-
+    )(vol, up, wl, bias)
+    act, ig, wg, bg = pl.pallas_call(
+        deliver,
+        out_shape=(
+            sds((SHARE, g.H, LANES), bf16),
+            sds((SHARE, g.H, LANES), bf16),
+            sds((27, SHARE, C), f32),
+            sds((1, SHARE), f32),
+        ),
+        in_specs=[hbm] * 4,
+        out_specs=(hbm,) * 4,
+        scratch_shapes=[dma((4,))],
+    )(act, ig, wg, bg)
     wgrad = jnp.transpose(wg.reshape(3, 3, 3, SHARE, C), (3, 4, 0, 1, 2))
-    return back(act), back(ig), wgrad, bg[:, g.KW % LANES]
-
-
-def solution(mesh, rows=48, halves=2, blocks=4):
+    return act[:, None], ig[:, None], wgrad, bg[0]
+
+
+def solution(mesh, rows=48, halves=2, blocks=8):
     planes, ranks = mesh.shape["space"], mesh.shape["chan"]
     factor = 1.0 / math.sqrt(planes * rows * LANES)
     g = Plan(planes, ranks, rows, halves, blocks, factor)

time: 59 us -> 65.1 us (1.10)
  Pallas kernels: 52.9 us -> 64.3 us
  local copies, waits for them, and re-layouts: 5.18 us -> 0 us
    pallas_call x1 -> x2, Pallas kernels: 52.9 us -> 64.3 us  [the longest x1 53.8 us: shards(): pl.pallas_call(functools.partial(kernel, g), out_shape=(sds((SHARE, g.H,...]
    unnamed x7 -> x0, local copies, waits for them, and re-layouts: 2.05 us -> none
    reshape x3 -> x0, local copies, waits for them, and re-layouts: 1.43 us -> none  [the longest x2 1.31 us: back(): return jnp.transpose(x.reshape(g.H, SHARE, LANES), (1, 0, 2))[:, None]]
    transpose x2 -> x0, local copies, waits for them, and re-layouts: 0.93 us -> none  [the longest x1 0.88 us: shards(): wl = jnp.transpose(weight, (3, 0, 2, 4, 1)).reshape(3, SHARE, g.KW)]
    slice x1 -> x0, local copies, waits for them, and re-layouts: 0.69 us -> none  [shards(): return (back(act), back(ig), wgrad, bg[:, g.KW % LANES])]
where the time goes in v2:
time: 65.1 us; the launch traced here: 64.9 us
  Pallas kernels  64.3 us (99%)
    pallas_call x1, Pallas kernels, shards(): pl.pallas_call(functools.partial(kernel, g), out_shape=(sds((SHARE, g.H,...  53.8 us
    pallas_call x1, Pallas kernels, shards(): pl.pallas_call(deliver, out_shape=(sds((SHARE, g.H, LANES), bf16), sds((S...  10.5 us

profile of v2, /device:TPU:1, one launch (start us, length us, event | category | flops | bytes accessed | tf_op | source)
XLA Modules:
  0.0 64.9 jit_solution(8399049884482184061)
XLA Ops:
  0.6 53.8 %shard_map.75 = (bf16[8,48,128]{2,1,0:T(8,128)(2,1)}, bf16[8,48,128]{2,1,0:T(8,128)(2,1)}, f32[27,8,64]{2,1,0:T(8,128)}, f32[1,8]{1,0:T(1,128)}) custom-call(bf16[8,48,128]{2,1,0:T(8,128)(2,1)} %bitcast.15, bf16[8,48,128]{2,1,0:T(8,128)(2,1)} %bitcast.16, bf16[27,8,64]{2,1,0:T(8,128)(2,1)} %bitcast.17, f32[8]{0:T(128)} %bias.1), custom_call_target="tpu_custom_call" | custom-call | tf_op jit(solution)/shard_map/pallas_call | solution.py:439
  54.4 10.5 %shard_map.76 = (bf16[8,48,128]{2,1,0:T(8,128)(2,1)}, bf16[8,48,128]{2,1,0:T(8,128)(2,1)}, f32[27,8,64]{2,1,0:T(8,128)}, f32[1,8]{1,0:T(1,128)}) custom-call(bf16[8,48,128]{2,1,0:T(8,128)(2,1)} %get-tuple-element.12.act, bf16[8,48,128]{2,1,0:T(8,128)(2,1)} %get-tuple-element.13.ig, f32[27,8,64]{2,1,0:T(8,128)} %get-tuple-element.14.wg, ...), custom_call_target="tpu_custom_call" | custom-call | tf_op jit(solution)/shard_map/pallas_call | solution.py:454

commit v3 on v2

--- a/solution.py
+++ b/solution.py
@@ -37,9 +37,9 @@
 def kernel(
     g, vol, up, wl, bias,
     act_o, ig_o, wg_o, bg_o,
-    RAW, RAWW, TALL, SEND, RCV, HV, XL, DX, DL, W1, W2, PRE, DB, AIS, AIR,
+    RAW, RAWW, TALL, SENDV, SENDW, RCVV, RCVW, HV, XL, DX, DL, W1, W2, PRE, DB, AIS, AIR,
     GT, GS, GR, SB, Q1, Q2, FIN, OUTS, OUTW, OUTB,
-    l_s, o_s, v_s, v_r, p_s, p_r, d_s, d_r, i_s, i_r,
+    l_s, o_s, v_s, v_r, w_s, w_r, far, p_s, p_r, d_s, d_r, i_s, i_r,
     g_s, g_r, q1_s, q1_r, q2_s, q2_r, q3_s, q3_r,
 ):
     N, Pn, R, C, M, B, U = g.N, g.P, g.R, g.C, g.M, g.B, g.U
@@ -91,14 +91,15 @@
         greet(s, chan_peer(k))
     for k in range(1, M):
         greet(group_peer(k)[1], r)
-    for k in range(1, B):
+    near = sorted({1, B - 1} - {0})
+    for k in near:
         greet(block_peer(k), r)
     for ds, dr in around:
         pl.when(inside(ds, dr))(functools.partial(greet, s + ds, r + dr))
     wide_s = 1 + jnp.where(s > 0, 1, 0) + jnp.where(s < N - 1, 1, 0)
     wide_r = 1 + jnp.where(r > 0, 1, 0) + jnp.where(r < Pn - 1, 1, 0)
 
-    V, Wt = R + 2, 2 * R + 2
+    V, Wt = R + 2, R
     loads = [
         pltpu.make_async_copy(vol, RAW.at[0], l_s.at[0]),
         pltpu.make_async_copy(up, RAW.at[1], l_s.at[1]),
@@ -125,28 +126,49 @@
         for j in range(g.NJ):
             part = whole[:, j * LANES : (j + 1) * LANES].astype(bf16)
             for to in range(Pn):
-                SEND[to, Wt + b * g.NJ + j] = part
+                SENDW[to, Wt + b * g.NJ + j] = part
     for n in range(2):
         TALL[n] = RAW[n].astype(f32).reshape(SHARE * g.H, LANES)
     zero_tile = jnp.zeros(tile, bf16)
-    SEND[0, 0] = zero_tile
-    SEND[Pn - 1, R + 1] = zero_tile
+    SENDV[0, 0] = zero_tile
+    SENDV[Pn - 1, R + 1] = zero_tile
     for h in range(g.H):
         row = TALL[0, pl.ds(h, SHARE, stride=g.H), :].astype(bf16)
         for to in range(Pn):
             if 0 <= h + 1 - R * to < V:
-                SEND[to, h + 1 - R * to] = row
-        SEND[h // R, V + h % R] = TALL[1, pl.ds(h, SHARE, stride=g.H), :].astype(bf16)
-
-    pl.semaphore_wait(barrier, (Pn - 1) + (M - 1) + (B - 1) + wide_s * wide_r - 1)
-
-    vsend = []
+                SENDV[to, h + 1 - R * to] = row
+        SENDW[h // R, h % R] = TALL[1, pl.ds(h, SHARE, stride=g.H), :].astype(bf16)
+
+    pl.semaphore_wait(barrier, (Pn - 1) + (M - 1) + len(near) + wide_s * wide_r - 1)
+
+    reach = [1 << i for i in range(8) if 1 << i < B // 2]
+
+    def relay(i):
+        if i < len(reach):
+            for k in sorted({reach[i], B - reach[i]}):
+                pl.semaphore_signal(
+                    far.at[i], inc=1, device_id=(block_peer(k), r), device_id_type=MESH
+                )
+
+    def heard(i):
+        if i < len(reach):
+            pl.semaphore_wait(far.at[i], len({reach[i], B - reach[i]}))
+
+    relay(0)
+
+    vsend, wsend = [], []
     for k in range(1, Pn):
         to = chan_peer(k)
-        c = copy(SEND.at[to], RCV.at[r], v_s.at[k], v_r.at[k], s, to)
+        c = copy(SENDV.at[to], RCVV.at[r], v_s.at[k], v_r.at[k], s, to)
         start(c)
         vsend.append(c)
-    RCV[r] = SEND[r]
+    for k in range(1, Pn):
+        to = chan_peer(k)
+        c = copy(SENDW.at[to], RCVW.at[r], w_s.at[k], w_r.at[k], s, to)
+        start(c)
+        wsend.append(c)
+    RCVV[r] = SENDV[r]
+    RCVW[r] = SENDW[r]
 
     def clear(ref, a):
         def body(i, _):
@@ -183,14 +205,15 @@
     for c in vsend:
         c.wait_recv()
 
-    mine = RCV.at[:, pl.ds(0, V)]
-    down = copy(mine, HV.at[1], p_s.at[0], p_r.at[0], s - 1, r)
-    upw = copy(mine, HV.at[0], p_s.at[1], p_r.at[1], s + 1, r)
+    down = copy(RCVV, HV.at[1], p_s.at[0], p_r.at[0], s - 1, r)
+    upw = copy(RCVV, HV.at[0], p_s.at[1], p_r.at[1], s + 1, r)
     pl.when(s > 0)(down.start)
     pl.when(s < N - 1)(upw.start)
     pending.append((s > 0, down))
     pending.append((s < N - 1, upw))
 
+    heard(0)
+    relay(1)
     last = pl.ds((g.NJ - 1) * LANES, LANES)
     lane = lax.broadcasted_iota(jnp.int32, (C, LANES), 1)
 
@@ -206,11 +229,13 @@
             return 0
         lax.fori_loop(0, R + 2, body, 0)
 
-    spread(lambda i: RCV[:, i], XL, 1)
-
+    spread(lambda i: RCVV[:, i], XL, 1)
+
+    for c in wsend:
+        c.wait_recv()
     for b in range(3):
         whole = jnp.concatenate(
-            [RCV[:, Wt + b * g.NJ + j].astype(f32).reshape(C, LANES) for j in range(g.NJ)], axis=1
+            [RCVW[:, Wt + b * g.NJ + j].astype(f32).reshape(C, LANES) for j in range(g.NJ)], axis=1
         )
         W1[b] = whole[:, : g.KW].astype(bf16)
         if b == 0:
@@ -240,7 +265,7 @@
         gate = jnp.where(p >= 0.0, 1.0, e) / (1.0 + e)
         act = leakage * p + (1.0 - leakage) * soft
         AIS[:, 0, j] = act.reshape(Pn, SHARE, LANES).astype(bf16)
-        u = RCV[:, V + j].astype(f32).reshape(C, LANES)
+        u = RCVW[:, j].astype(f32).reshape(C, LANES)
         d = (u * (leakage + (1.0 - leakage) * gate)).astype(bf16)
         DX[1, 1 + j] = d
         DB[:, pl.ds(j * LANES, LANES)] = d
@@ -330,6 +355,7 @@
     for m in range(1, M):
         acc = acc + Q1[m]
     Q2[block] = acc
+    heard(1)
     q2send = []
     for k in range(1, B):
         c = copy(Q2.at[block], Q2.at[block], q2_s.at[k], q2_r.at[k], block_peer(k), r)
@@ -381,13 +407,18 @@
         c.wait()
 
 
-def deliver(act, ig, wg, bg, act_o, ig_o, wg_o, bg_o, sems):
-    pairs = ((act, act_o), (ig, ig_o), (wg, wg_o), (bg, bg_o))
-    moves = [pltpu.make_async_copy(a, b, sems.at[i]) for i, (a, b) in enumerate(pairs)]
-    for c in moves:
+def deliver(act, ig, wg, bg, act_o, ig_o, wg_o, bg_o, act_v, ig_v, wg_v, bg_v, i_s, o_s):
+    held = (act_v, ig_v, wg_v, bg_v)
+    ins = [pltpu.make_async_copy(a, v, i_s.at[n]) for n, (a, v) in enumerate(zip((act, ig, wg, bg), held))]
+    outs = (act_o, ig_o, wg_o, bg_o)
+    outs = [pltpu.make_async_copy(v, b, o_s.at[n]) for n, (v, b) in enumerate(zip(held, outs))]
+    for c in ins:
         c.start()
-    for c in moves:
+    for c, d in zip(ins, outs):
         c.wait()
+        d.start()
+    for d in outs:
+        d.wait()
 
 
 def shards(g, volume, weight, bias, upstream):
@@ -404,8 +435,10 @@
         V((2, SHARE, g.H, LANES), bf16),
         V((27, SHARE, C), bf16),
         V((2, SHARE * g.H, LANES), f32),
-        V((Pn, 2 * R + 2 + 3 * g.NJ, SHARE, LANES), bf16),
-        V((Pn, 2 * R + 2 + 3 * g.NJ, SHARE, LANES), bf16),
+        V((Pn, R + 2, SHARE, LANES), bf16),
+        V((Pn, R + 3 * g.NJ, SHARE, LANES), bf16),
+        V((Pn, R + 2, SHARE, LANES), bf16),
+        V((Pn, R + 3 * g.NJ, SHARE, LANES), bf16),
         V((2, Pn, R + 2, SHARE, LANES), bf16),
         V((9 * C, rows), bf16),
         V((3, R + 2, C, LANES), bf16),
@@ -428,7 +461,8 @@
         V((1, SHARE), f32),
         dma((3,)),
         dma((4,)),
-        *chan,
+        *chan, *chan,
+        pltpu.SemaphoreType.REGULAR((2,)),
         dma((2,)), dma((2,)),
         dma((8,)), dma((8,)),
         *chan, *chan,
@@ -461,7 +495,14 @@
         ),
         in_specs=[hbm] * 4,
         out_specs=(hbm,) * 4,
-        scratch_shapes=[dma((4,))],
+        scratch_shapes=[
+            V((SHARE, g.H, LANES), bf16),
+            V((SHARE, g.H, LANES), bf16),
+            V((27, SHARE, C), f32),
+            V((1, SHARE), f32),
+            dma((4,)),
+            dma((4,)),
+        ],
     )(act, ig, wg, bg)
     wgrad = jnp.transpose(wg.reshape(3, 3, 3, SHARE, C), (3, 4, 0, 1, 2))
     return act[:, None], ig[:, None], wgrad, bg[0]

time: 65.1 us -> 54.1 us (0.83)
  Pallas kernels: 64.3 us -> 53.3 us
    pallas_call x1, Pallas kernels: 10.5 us -> 1.71 us  [shards(): pl.pallas_call(deliver, out_shape=(sds((SHARE, g.H, LANES), bf16), sds((S...]
    pallas_call x1, Pallas kernels: 53.8 us -> 51.6 us  [shards(): pl.pallas_call(functools.partial(kernel, g), out_shape=(sds((SHARE, g.H,...]
where the time goes in v3:
time: 54.1 us; the launch traced here: 53.9 us
  Pallas kernels  53.3 us (99%)
  between operations  0.64 us (1%)
    pallas_call x1, Pallas kernels, shards(): pl.pallas_call(functools.partial(kernel, g), out_shape=(sds((SHARE, g.H,...  51.6 us
    pallas_call x1, Pallas kernels, shards(): pl.pallas_call(deliver, out_shape=(sds((SHARE, g.H, LANES), bf16), sds((S...  1.71 us

profile of v3, /device:TPU:1, one launch (start us, length us, event | category | flops | bytes accessed | tf_op | source)
XLA Modules:
  0.0 53.9 jit_solution(10105481115311648729)
XLA Ops:
  0.6 51.6 %shard_map.75 = (bf16[8,48,128]{2,1,0:T(8,128)(2,1)}, bf16[8,48,128]{2,1,0:T(8,128)(2,1)}, f32[27,8,64]{2,1,0:T(8,128)}, f32[1,8]{1,0:T(1,128)}) custom-call(bf16[8,48,128]{2,1,0:T(8,128)(2,1)} %bitcast.15, bf16[8,48,128]{2,1,0:T(8,128)(2,1)} %bitcast.16, bf16[27,8,64]{2,1,0:T(8,128)(2,1)} %bitcast.17, f32[8]{0:T(128)} %bias.1), custom_call_target="tpu_custom_call" | custom-call | tf_op jit(solution)/shard_map/pallas_call | solution.py:473
  52.2 1.7 %shard_map.76 = (bf16[8,48,128]{2,1,0:T(8,128)(2,1)}, bf16[8,48,128]{2,1,0:T(8,128)(2,1)}, f32[27,8,64]{2,1,0:T(8,128)}, f32[1,8]{1,0:T(1,128)}) custom-call(bf16[8,48,128]{2,1,0:T(8,128)(2,1)} %get-tuple-element.12.act, bf16[8,48,128]{2,1,0:T(8,128)(2,1)} %get-tuple-element.13.ig, f32[27,8,64]{2,1,0:T(8,128)} %get-tuple-element.14.wg, ...), custom_call_target="tpu_custom_call" | custom-call | tf_op jit(solution)/shard_map/pallas_call | solution.py:488

commit v4 on v3

--- a/solution.py
+++ b/solution.py
@@ -37,7 +37,7 @@
 def kernel(
     g, vol, up, wl, bias,
     act_o, ig_o, wg_o, bg_o,
-    RAW, RAWW, TALL, SENDV, SENDW, RCVV, RCVW, HV, XL, DX, DL, W1, W2, PRE, DB, AIS, AIR,
+    RAW, RAWW, RAWB, TALL, SENDV, SENDW, RCVV, RCVW, HV, XL, DX, DL, W1, WA, W2, PRE, DB, AIS, AIR,
     GT, GS, GR, SB, Q1, Q2, FIN, OUTS, OUTW, OUTB,
     l_s, o_s, v_s, v_r, w_s, w_r, far, p_s, p_r, d_s, d_r, i_s, i_r,
     g_s, g_r, q1_s, q1_r, q2_s, q2_r, q3_s, q3_r,
@@ -104,6 +104,7 @@
         pltpu.make_async_copy(vol, RAW.at[0], l_s.at[0]),
         pltpu.make_async_copy(up, RAW.at[1], l_s.at[1]),
         pltpu.make_async_copy(wl, RAWW, l_s.at[2]),
+        pltpu.make_async_copy(bias, RAWB, l_s.at[3]),
     ]
     for c in loads:
         c.start()
@@ -115,7 +116,7 @@
     col = lax.broadcasted_iota(jnp.int32, (SHARE, g.KP - g.KW), 1)
     b0 = jnp.zeros((SHARE, g.KP - g.KW), f32)
     for q in range(SHARE):
-        b0 = jnp.where(sub == q, bias[q], b0)
+        b0 = jnp.where(sub == q, RAWB[0, q], b0)
     hi = b0.astype(bf16).astype(f32)
     mid = (b0 - hi).astype(bf16).astype(f32)
     low = (b0 - hi - mid).astype(bf16).astype(f32)
@@ -156,18 +157,22 @@
 
     relay(0)
 
+    RCVV[r] = SENDV[r]
+
+    def nearness(k):
+        return k % 2, min(k, Pn - k)
+
     vsend, wsend = [], []
-    for k in range(1, Pn):
+    for k in sorted(range(1, Pn), key=nearness, reverse=True):
         to = chan_peer(k)
         c = copy(SENDV.at[to], RCVV.at[r], v_s.at[k], v_r.at[k], s, to)
         start(c)
-        vsend.append(c)
+        vsend.append((k, c))
     for k in range(1, Pn):
         to = chan_peer(k)
         c = copy(SENDW.at[to], RCVW.at[r], w_s.at[k], w_r.at[k], s, to)
         start(c)
         wsend.append(c)
-    RCVV[r] = SENDV[r]
     RCVW[r] = SENDW[r]
 
     def clear(ref, a):
@@ -202,15 +207,20 @@
         for a in range(3):
             DX[a, R + 1] = jnp.zeros((C, LANES), bf16)
 
-    for c in vsend:
-        c.wait_recv()
-
-    down = copy(RCVV, HV.at[1], p_s.at[0], p_r.at[0], s - 1, r)
-    upw = copy(RCVV, HV.at[0], p_s.at[1], p_r.at[1], s + 1, r)
-    pl.when(s > 0)(down.start)
-    pl.when(s < N - 1)(upw.start)
-    pending.append((s > 0, down))
-    pending.append((s < N - 1, upw))
+    halo = [[], []]
+
+    def forward(k):
+        q = lax.rem(r + Pn - k, Pn)
+        for n, (ok, to) in enumerate(((s > 0, s - 1), (s < N - 1, s + 1))):
+            c = copy(RCVV.at[q], HV.at[1 - n, q], p_s.at[n, k], p_r.at[n, k], to, r)
+            pl.when(ok)(c.start)
+            pending.append((ok, c))
+            halo[n].append(c)
+
+    forward(0)
+    for k, c in sorted(vsend, key=lambda kc: nearness(kc[0])):
+        c.wait_recv()
+        forward(k)
 
     heard(0)
     relay(1)
@@ -238,15 +248,12 @@
             [RCVW[:, Wt + b * g.NJ + j].astype(f32).reshape(C, LANES) for j in range(g.NJ)], axis=1
         )
         W1[b] = whole[:, : g.KW].astype(bf16)
+        for a in range(3):
+            WA[a, b] = whole[:, a * 3 * C : (a + 1) * 3 * C].astype(bf16)
         if b == 0:
             end = whole[:, g.KP - LANES :]
             own = jnp.logical_and(lane >= edge, lane < edge + 3)
             bcol = jnp.sum(jnp.where(own, end, 0.0), axis=1, keepdims=True)
-
-    pl.when(s < N - 1)(down.wait_recv)
-    pl.when(s > 0)(upw.wait_recv)
-    spread(lambda i: HV[0, :, i], XL, 0)
-    spread(lambda i: HV[1, :, i], XL, 2)
 
     def conv(w, x):
         acc = None
@@ -255,7 +262,25 @@
             acc = part if acc is None else acc + part
         return acc
 
-    PRE[...] = conv(W1, XL)
+    def third(a):
+        acc = None
+        for b in range(3):
+            x = XL[pl.ds(a * 3 * C, 3 * C), pl.ds(b * LANES, R * LANES)]
+            part = jnp.dot(WA[a, b], x, preferred_element_type=f32)
+            acc = part if acc is None else acc + part
+        return acc
+
+    PRE[...] = third(1)
+    for n, ok in enumerate((s < N - 1, s > 0)):
+        @pl.when(ok)
+        def _(n=n):
+            for c in halo[n]:
+                c.wait_recv()
+
+    spread(lambda i: HV[0, :, i], XL, 0)
+    spread(lambda i: HV[1, :, i], XL, 2)
+
+    PRE[...] = PRE[...] + third(0) + third(2)
 
     dsum = jnp.zeros((C, LANES), f32)
     for j in range(R):
@@ -434,6 +459,7 @@
     scratch = [
         V((2, SHARE, g.H, LANES), bf16),
         V((27, SHARE, C), bf16),
+        pltpu.SMEM((1, SHARE), f32),
         V((2, SHARE * g.H, LANES), f32),
         V((Pn, R + 2, SHARE, LANES), bf16),
         V((Pn, R + 3 * g.NJ, SHARE, LANES), bf16),
@@ -444,6 +470,7 @@
         V((3, R + 2, C, LANES), bf16),
         V((9 * C, rows), bf16),
         V((3, C, g.KW), bf16),
+        V((3, 3, C, 3 * C), bf16),
         V((3, C, g.KW), bf16),
         V((C, R * LANES), f32),
         V((C, R * LANES), bf16),
@@ -459,11 +486,11 @@
         V((2, SHARE, g.H, LANES), bf16),
         V((27, SHARE, C), f32),
         V((1, SHARE), f32),
-        dma((3,)),
+        dma((4,)),
         dma((4,)),
         *chan, *chan,
         pltpu.SemaphoreType.REGULAR((2,)),
-        dma((2,)), dma((2,)),
+        dma((2, Pn)), dma((2, Pn)),
         dma((8,)), dma((8,)),
         *chan, *chan,
         dma((M,)), dma((M,)),
@@ -478,13 +505,13 @@
             sds((27, SHARE, C), f32),
             sds((1, SHARE), f32),
         ),
-        in_specs=[hbm, hbm, hbm, pl.BlockSpec(memory_space=pltpu.SMEM)],
+        in_specs=[hbm] * 4,
         out_specs=(hbm,) * 4,
         scratch_shapes=scratch,
         compiler_params=pltpu.CompilerParams(
             collective_id=0, has_side_effects=True, vmem_limit_bytes=62 << 20
         ),
-    )(vol, up, wl, bias)
+    )(vol, up, wl, bias[None])
     act, ig, wg, bg = pl.pallas_call(
         deliver,
         out_shape=(

time: 54.1 us -> 52.9 us (0.978)
  Pallas kernels: 53.3 us -> 52.1 us
    pallas_call x1, Pallas kernels: 51.6 us -> 50.4 us  [shards(): pl.pallas_call(functools.partial(kernel, g), out_shape=(sds((SHARE, g.H,...]
where the time goes in v4:
time: 52.9 us; the launch traced here: 52.7 us
  Pallas kernels  52.1 us (98%)
  between operations  0.64 us (1%)
    pallas_call x1, Pallas kernels, shards(): pl.pallas_call(functools.partial(kernel, g), out_shape=(sds((SHARE, g.H,...  50.4 us
    pallas_call x1, Pallas kernels, shards(): pl.pallas_call(deliver, out_shape=(sds((SHARE, g.H, LANES), bf16), sds((S...  1.71 us

profile of v4, /device:TPU:1, one launch (start us, length us, event | category | flops | bytes accessed | tf_op | source)
XLA Modules:
  0.0 52.7 jit_solution(13553130722839397530)
XLA Ops:
  0.6 50.4 %shard_map.75 = (bf16[8,48,128]{2,1,0:T(8,128)(2,1)}, bf16[8,48,128]{2,1,0:T(8,128)(2,1)}, f32[27,8,64]{2,1,0:T(8,128)}, f32[1,8]{1,0:T(1,128)}) custom-call(bf16[8,48,128]{2,1,0:T(8,128)(2,1)} %bitcast.16, bf16[8,48,128]{2,1,0:T(8,128)(2,1)} %bitcast.17, bf16[27,8,64]{2,1,0:T(8,128)(2,1)} %bitcast.18, f32[1,8]{1,0:T(1,128)} %bitcast.19), custom_call_target="tpu_custom_call" | custom-call | tf_op jit(solution)/shard_map/pallas_call | solution.py:500
  51.0 1.7 %shard_map.76 = (bf16[8,48,128]{2,1,0:T(8,128)(2,1)}, bf16[8,48,128]{2,1,0:T(8,128)(2,1)}, f32[27,8,64]{2,1,0:T(8,128)}, f32[1,8]{1,0:T(1,128)}) custom-call(bf16[8,48,128]{2,1,0:T(8,128)(2,1)} %get-tuple-element.12.act, bf16[8,48,128]{2,1,0:T(8,128)(2,1)} %get-tuple-element.13.ig, f32[27,8,64]{2,1,0:T(8,128)} %get-tuple-element.14.wg, ...), custom_call_target="tpu_custom_call" | custom-call | tf_op jit(solution)/shard_map/pallas_call | solution.py:515

commit v5 on v4

--- a/solution.py
+++ b/solution.py
@@ -38,8 +38,8 @@
     g, vol, up, wl, bias,
     act_o, ig_o, wg_o, bg_o,
     RAW, RAWW, RAWB, TALL, SENDV, SENDW, RCVV, RCVW, HV, XL, DX, DL, W1, WA, W2, PRE, DB, AIS, AIR,
-    GT, GS, GR, SB, Q1, Q2, FIN, OUTS, OUTW, OUTB,
-    l_s, o_s, v_s, v_r, w_s, w_r, far, p_s, p_r, d_s, d_r, i_s, i_r,
+    GT, GS, GR, SB, Q1, Q2, FIN,
+    l_s, v_s, v_r, w_s, w_r, far, p_s, p_r, d_s, d_r, i_s, i_r,
     g_s, g_r, q1_s, q1_r, q2_s, q2_r, q3_s, q3_r,
 ):
     N, Pn, R, C, M, B, U = g.N, g.P, g.R, g.C, g.M, g.B, g.U
@@ -297,6 +297,7 @@
         dsum = dsum + d.astype(f32)
 
     dcol = jnp.sum(dsum, axis=1, keepdims=True)
+    gsend = []
     for b in range(3):
         GT[b, :, pl.ds(0, g.KW)] = lax.dot_general(
             DB[...], XL[:, pl.ds(b * LANES, R * LANES)],
@@ -308,14 +309,15 @@
             cur = jnp.where(lane == edge, dcol, cur)
         GT[b, :, last] = cur
         for to in range(Pn):
-            GS[to, b] = GT[b, pl.ds(SHARE * to, SHARE), :].astype(GS.dtype)
-    gsend = []
-    for k in range(1, Pn):
-        to = chan_peer(k)
-        c = copy(GS.at[to], GR.at[r], g_s.at[k], g_r.at[k], s, to)
-        start(c)
-        gsend.append(c)
-    GR[r] = GS[r]
+            GS[b, to] = GT[b, pl.ds(SHARE * to, SHARE), :].astype(GS.dtype)
+        sent = []
+        for k in sorted(range(1, Pn), key=nearness, reverse=True):
+            to = chan_peer(k)
+            c = copy(GS.at[b, to], GR.at[b, r], g_s.at[b, k], g_r.at[b, k], s, to)
+            start(c)
+            sent.append(c)
+        gsend.append(sent)
+        GR[b, r] = GS[b, r]
 
     dcopies = []
     for e, (ds, dr) in enumerate(around):
@@ -339,12 +341,12 @@
                 blocks.append(whole[at : at + C])
         W2[b] = jnp.concatenate(blocks, axis=1).astype(bf16)
 
-    for c in gsend:
-        c.wait_recv()
     for b in range(3):
-        acc = GR[0, b].astype(f32)
+        for c in gsend[b]:
+            c.wait_recv()
+        acc = GR[b, 0].astype(f32)
         for q in range(1, Pn):
-            acc = acc + GR[q, b].astype(f32)
+            acc = acc + GR[b, q].astype(f32)
         for j in range(g.NJ):
             t = b * g.NJ + j
             SB[t // g.T, t % g.T] = acc[:, j * LANES : (j + 1) * LANES]
@@ -388,13 +390,10 @@
         q2send.append(c)
     for c in isend:
         c.wait_recv()
-    leave = []
     for n, out in enumerate((act_o, ig_o)):
         TALL[n] = AIR[:, n].astype(f32).reshape(g.H * SHARE, LANES)
         for q in range(SHARE):
-            OUTS[n, q] = TALL[n, pl.ds(q, g.H, stride=SHARE), :].astype(bf16)
-        leave.append(pltpu.make_async_copy(OUTS.at[n], out, o_s.at[n]))
-        leave[n].start()
+            out[q] = TALL[n, pl.ds(q, g.H, stride=SHARE), :].astype(bf16)
     for c in q2send:
         c.wait_recv()
     acc = Q2[0]
@@ -414,36 +413,26 @@
                 at = (a * 3 + c_) * C
                 t = b * g.NJ + at // LANES
                 off = at % LANES
-                OUTW[(a * 3 + b) * 3 + c_] = FIN[t // g.T, t % g.T][:, off : off + C]
+                wg_o[(a * 3 + b) * 3 + c_] = FIN[t // g.T, t % g.T][:, off : off + C]
     t = g.NJ - 1
     sums = FIN[t // g.T, t % g.T][:, edge : edge + 1]
     spot = lax.broadcasted_iota(jnp.int32, tile, 0) == lax.broadcasted_iota(jnp.int32, tile, 1)
-    OUTB[...] = jnp.sum(jnp.where(spot, sums, 0.0), axis=0, keepdims=True)[:, :SHARE]
-    for n, (a, b) in enumerate(((OUTW, wg_o), (OUTB, bg_o))):
-        leave.append(pltpu.make_async_copy(a, b, o_s.at[2 + n]))
-        leave[-1].start()
+    bg_o[...] = jnp.sum(jnp.where(spot, sums, 0.0), axis=0, keepdims=True)[:, :SHARE]
 
     for ok, c in pending:
         if ok is None:
             c.wait_send()
         else:
             pl.when(ok)(c.wait_send)
-    for c in leave:
+
+
+def deliver(act, ig, wg, bg, act_o, ig_o, wg_o, bg_o, sems):
+    pairs = ((act, act_o), (ig, ig_o), (wg, wg_o), (bg, bg_o))
+    moves = [pltpu.make_async_copy(a, b, sems.at[n]) for n, (a, b) in enumerate(pairs)]
+    for c in moves:
+        c.start()
+    for c in moves:
         c.wait()
-
-
-def deliver(act, ig, wg, bg, act_o, ig_o, wg_o, bg_o, act_v, ig_v, wg_v, bg_v, i_s, o_s):
-    held = (act_v, ig_v, wg_v, bg_v)
-    ins = [pltpu.make_async_copy(a, v, i_s.at[n]) for n, (a, v) in enumerate(zip((act, ig, wg, bg), held))]
-    outs = (act_o, ig_o, wg_o, bg_o)
-    outs = [pltpu.make_async_copy(v, b, o_s.at[n]) for n, (v, b) in enumerate(zip(held, outs))]
-    for c in ins:
-        c.start()
-    for c, d in zip(ins, outs):
-        c.wait()
-        d.start()
-    for d in outs:
-        d.wait()
 
 
 def shards(g, volume, weight, bias, upstream):
@@ -477,22 +466,19 @@
         V((Pn, 2, R, SHARE, LANES), bf16),
         V((Pn, 2, R, SHARE, LANES), bf16),
         V((3, C, g.KP), f32),
-        V((Pn, 3, SHARE, g.KP), bf16),
-        V((Pn, 3, SHARE, g.KP), bf16),
+        V((3, Pn, SHARE, g.KP), bf16),
+        V((3, Pn, SHARE, g.KP), bf16),
         V((M, g.T, SHARE, LANES), f32),
         V((M, g.T, SHARE, LANES), f32),
         V((B, g.T, SHARE, LANES), f32),
         V((M, g.T, SHARE, LANES), f32),
-        V((2, SHARE, g.H, LANES), bf16),
-        V((27, SHARE, C), f32),
-        V((1, SHARE), f32),
-        dma((4,)),
         dma((4,)),
         *chan, *chan,
         pltpu.SemaphoreType.REGULAR((2,)),
         dma((2, Pn)), dma((2, Pn)),
         dma((8,)), dma((8,)),
-        *chan, *chan,
+        *chan,
+        dma((3, Pn)), dma((3, Pn)),
         dma((M,)), dma((M,)),
         dma((B,)), dma((B,)),
         dma((M,)), dma((M,)),
@@ -506,12 +492,12 @@
             sds((1, SHARE), f32),
         ),
         in_specs=[hbm] * 4,
-        out_specs=(hbm,) * 4,
+        out_specs=(pl.BlockSpec(memory_space=pltpu.VMEM),) * 4,
         scratch_shapes=scratch,
         compiler_params=pltpu.CompilerParams(
-            collective_id=0, has_side_effects=True, vmem_limit_bytes=62 << 20
+            collective_id=0, has_side_effects=True, vmem_limit_bytes=40 << 20
         ),
-    )(vol, up, wl, bias[None])
+    )(*(pltpu.with_memory_space_constraint(x, pltpu.HBM) for x in (vol, up, wl, bias[None])))
     act, ig, wg, bg = pl.pallas_call(
         deliver,
         out_shape=(
@@ -520,16 +506,10 @@
             sds((27, SHARE, C), f32),
             sds((1, SHARE), f32),
         ),
-        in_specs=[hbm] * 4,
+        in_specs=[pl.BlockSpec(memory_space=pl.ANY)] * 4,
         out_specs=(hbm,) * 4,
-        scratch_shapes=[
-            V((SHARE, g.H, LANES), bf16),
-            V((SHARE, g.H, LANES), bf16),
-            V((27, SHARE, C), f32),
-            V((1, SHARE), f32),
-            dma((4,)),
-            dma((4,)),
-        ],
+        scratch_shapes=[dma((4,))],
+        compiler_params=pltpu.CompilerParams(vmem_limit_bytes=1 << 20),
     )(act, ig, wg, bg)
     wgrad = jnp.transpose(wg.reshape(3, 3, 3, SHARE, C), (3, 4, 0, 1, 2))
     return act[:, None], ig[:, None], wgrad, bg[0]

time: 52.9 us -> 51.7 us (0.977)
  Pallas kernels: 52.1 us -> 50.9 us
    pallas_call x1, Pallas kernels: 1.71 us -> 0.75 us  [shards(): pl.pallas_call(deliver, out_shape=(sds((SHARE, g.H, LANES), bf16), sds((S...]
where the time goes in v5:
time: 51.7 us; the launch traced here: 51.6 us
  Pallas kernels  50.9 us (98%)
  between operations  0.64 us (1%)
    pallas_call x1, Pallas kernels, shards(): pl.pallas_call(functools.partial(kernel, g), out_shape=(sds((SHARE, g.H,...  50.2 us

profile of v5, /device:TPU:1, one launch (start us, length us, event | category | flops | bytes accessed | tf_op | source)
XLA Modules:
  0.0 51.6 jit_solution(17226902555805225788)
XLA Ops:
  0.6 50.2 %shard_map.75 = (bf16[8,48,128]{2,1,0:T(8,128)(2,1)S(1)}, bf16[8,48,128]{2,1,0:T(8,128)(2,1)S(1)}, f32[27,8,64]{2,1,0:T(8,128)S(1)}, f32[1,8]{1,0:T(1,128)S(1)}) custom-call(bf16[8,48,128]{2,1,0:T(8,128)(2,1)} %bitcast.16, bf16[8,48,128]{2,1,0:T(8,128)(2,1)} %bitcast.17, bf16[27,8,64]{2,1,0:T(8,128)(2,1)} %bitcast.18, f32[1,8]{1,0:T(1,128)} %bitcast.19), custom_call_target="tpu_custom_call" | custom-call | tf_op jit(solution)/shard_map/pallas_call | solution.py:486
  50.8 0.7 %shard_map.76 = (bf16[8,48,128]{2,1,0:T(8,128)(2,1)}, bf16[8,48,128]{2,1,0:T(8,128)(2,1)}, f32[27,8,64]{2,1,0:T(8,128)}, f32[1,8]{1,0:T(1,128)}) custom-call(bf16[8,48,128]{2,1,0:T(8,128)(2,1)S(1)} %get-tuple-element.12.act, bf16[8,48,128]{2,1,0:T(8,128)(2,1)S(1)} %get-tuple-element.13.ig, f32[27,8,64]{2,1,0:T(8,128)S(1)} %get-tuple-element.14.wg, ...), custom_call_target="tpu_custom_call" | custom-call | tf_op jit(solution)/shard_map/pallas_call | solution.py:501

commit v6 on v5

--- a/solution.py
+++ b/solution.py
@@ -364,6 +364,18 @@
         pl.when(ok)(c.wait_recv)
     for a in range(3):
         spread(lambda i, a=a: DX[a, i], DL, a)
+    for c in q1send:
+        c.wait_recv()
+    acc = Q1[0]
+    for m in range(1, M):
+        acc = acc + Q1[m]
+    Q2[block] = acc
+    heard(1)
+    q2send = []
+    for k in sorted(range(1, B), key=lambda k: -min(k, B - k)):
+        c = copy(Q2.at[block], Q2.at[block], q2_s.at[k], q2_r.at[k], block_peer(k), r)
+        start(c)
+        q2send.append(c)
     PRE[...] = conv(W2, DL)
     for j in range(R):
         v = PRE[:, pl.ds(j * LANES, LANES)]
@@ -376,24 +388,6 @@
         isend.append(c)
     AIR[r] = AIS[r]
 
-    for c in q1send:
-        c.wait_recv()
-    acc = Q1[0]
-    for m in range(1, M):
-        acc = acc + Q1[m]
-    Q2[block] = acc
-    heard(1)
-    q2send = []
-    for k in range(1, B):
-        c = copy(Q2.at[block], Q2.at[block], q2_s.at[k], q2_r.at[k], block_peer(k), r)
-        start(c)
-        q2send.append(c)
-    for c in isend:
-        c.wait_recv()
-    for n, out in enumerate((act_o, ig_o)):
-        TALL[n] = AIR[:, n].astype(f32).reshape(g.H * SHARE, LANES)
-        for q in range(SHARE):
-            out[q] = TALL[n, pl.ds(q, g.H, stride=SHARE), :].astype(bf16)
     for c in q2send:
         c.wait_recv()
     acc = Q2[0]
@@ -405,6 +399,12 @@
         c = copy(FIN.at[member], FIN.at[member], q3_s.at[k], q3_r.at[k], group_peer(k)[1], r)
         start(c)
         q3send.append(c)
+    for c in isend:
+        c.wait_recv()
+    for n, out in enumerate((act_o, ig_o)):
+        TALL[n] = AIR[:, n].astype(f32).reshape(g.H * SHARE, LANES)
+        for q in range(SHARE):
+            out[q] = TALL[n, pl.ds(q, g.H, stride=SHARE), :].astype(bf16)
     for c in q3send:
         c.wait_recv()
     for a in range(3):

time: 51.7 us -> 51.1 us (0.988)
  Pallas kernels: 50.9 us -> 50.3 us
    pallas_call x1, Pallas kernels: 50.2 us -> 49.5 us  [shards(): pl.pallas_call(functools.partial(kernel, g), out_shape=(sds((SHARE, g.H,...]
where the time goes in v6:
time: 51.1 us; the launch traced here: 50.9 us
  Pallas kernels  50.3 us (98%)
  between operations  0.64 us (1%)
    pallas_call x1, Pallas kernels, shards(): pl.pallas_call(functools.partial(kernel, g), out_shape=(sds((SHARE, g.H,...  49.5 us

profile of v6, /device:TPU:1, one launch (start us, length us, event | category | flops | bytes accessed | tf_op | source)
XLA Modules:
  0.0 50.9 jit_solution(6068138746426693363)
XLA Ops:
  0.6 49.5 %shard_map.75 = (bf16[8,48,128]{2,1,0:T(8,128)(2,1)S(1)}, bf16[8,48,128]{2,1,0:T(8,128)(2,1)S(1)}, f32[27,8,64]{2,1,0:T(8,128)S(1)}, f32[1,8]{1,0:T(1,128)S(1)}) custom-call(bf16[8,48,128]{2,1,0:T(8,128)(2,1)} %bitcast.16, bf16[8,48,128]{2,1,0:T(8,128)(2,1)} %bitcast.17, bf16[27,8,64]{2,1,0:T(8,128)(2,1)} %bitcast.18, f32[1,8]{1,0:T(1,128)} %bitcast.19), custom_call_target="tpu_custom_call" | custom-call | tf_op jit(solution)/shard_map/pallas_call | solution.py:486
  50.2 0.7 %shard_map.76 = (bf16[8,48,128]{2,1,0:T(8,128)(2,1)}, bf16[8,48,128]{2,1,0:T(8,128)(2,1)}, f32[27,8,64]{2,1,0:T(8,128)}, f32[1,8]{1,0:T(1,128)}) custom-call(bf16[8,48,128]{2,1,0:T(8,128)(2,1)S(1)} %get-tuple-element.12.act, bf16[8,48,128]{2,1,0:T(8,128)(2,1)S(1)} %get-tuple-element.13.ig, f32[27,8,64]{2,1,0:T(8,128)S(1)} %get-tuple-element.14.wg, ...), custom_call_target="tpu_custom_call" | custom-call | tf_op jit(solution)/shard_map/pallas_call | solution.py:501

commit v7 on v6

--- a/solution.py
+++ b/solution.py
@@ -37,9 +37,9 @@
 def kernel(
     g, vol, up, wl, bias,
     act_o, ig_o, wg_o, bg_o,
-    RAW, RAWW, RAWB, TALL, SENDV, SENDW, RCVV, RCVW, HV, XL, DX, DL, W1, WA, W2, PRE, DB, AIS, AIR,
+    RAW, RAWW, RAWB, TALL, SENDV, SENDU, SENDW, RCVV, RCVU, RCVW, HV, XL, DX, DL, W1, WA, W2, PRE, DB, AIS, AIR,
     GT, GS, GR, SB, Q1, Q2, FIN,
-    l_s, v_s, v_r, w_s, w_r, far, p_s, p_r, d_s, d_r, i_s, i_r,
+    l_s, v_s, v_r, w_s, w_r, u_s, u_r, far, p_s, p_r, d_s, d_r, i_s, i_r,
     g_s, g_r, q1_s, q1_r, q2_s, q2_r, q3_s, q3_r,
 ):
     N, Pn, R, C, M, B, U = g.N, g.P, g.R, g.C, g.M, g.B, g.U
@@ -99,7 +99,7 @@
     wide_s = 1 + jnp.where(s > 0, 1, 0) + jnp.where(s < N - 1, 1, 0)
     wide_r = 1 + jnp.where(r > 0, 1, 0) + jnp.where(r < Pn - 1, 1, 0)
 
-    V, Wt = R + 2, R
+    V = R + 2
     loads = [
         pltpu.make_async_copy(vol, RAW.at[0], l_s.at[0]),
         pltpu.make_async_copy(up, RAW.at[1], l_s.at[1]),
@@ -127,7 +127,7 @@
         for j in range(g.NJ):
             part = whole[:, j * LANES : (j + 1) * LANES].astype(bf16)
             for to in range(Pn):
-                SENDW[to, Wt + b * g.NJ + j] = part
+                SENDW[to, b * g.NJ + j] = part
     for n in range(2):
         TALL[n] = RAW[n].astype(f32).reshape(SHARE * g.H, LANES)
     zero_tile = jnp.zeros(tile, bf16)
@@ -138,7 +138,7 @@
         for to in range(Pn):
             if 0 <= h + 1 - R * to < V:
                 SENDV[to, h + 1 - R * to] = row
-        SENDW[h // R, h % R] = TALL[1, pl.ds(h, SHARE, stride=g.H), :].astype(bf16)
+        SENDU[h // R, h % R] = TALL[1, pl.ds(h, SHARE, stride=g.H), :].astype(bf16)
 
     pl.semaphore_wait(barrier, (Pn - 1) + (M - 1) + len(near) + wide_s * wide_r - 1)
 
@@ -174,6 +174,7 @@
         start(c)
         wsend.append(c)
     RCVW[r] = SENDW[r]
+    RCVU[r] = SENDU[r]
 
     def clear(ref, a):
         def body(i, _):
@@ -221,6 +222,13 @@
     for k, c in sorted(vsend, key=lambda kc: nearness(kc[0])):
         c.wait_recv()
         forward(k)
+
+    usend = []
+    for k in sorted(range(1, Pn), key=nearness, reverse=True):
+        to = chan_peer(k)
+        c = copy(SENDU.at[to], RCVU.at[r], u_s.at[k], u_r.at[k], s, to)
+        start(c)
+        usend.append(c)
 
     heard(0)
     relay(1)
@@ -245,7 +253,7 @@
         c.wait_recv()
     for b in range(3):
         whole = jnp.concatenate(
-            [RCVW[:, Wt + b * g.NJ + j].astype(f32).reshape(C, LANES) for j in range(g.NJ)], axis=1
+            [RCVW[:, b * g.NJ + j].astype(f32).reshape(C, LANES) for j in range(g.NJ)], axis=1
         )
         W1[b] = whole[:, : g.KW].astype(bf16)
         for a in range(3):
@@ -282,6 +290,8 @@
 
     PRE[...] = PRE[...] + third(0) + third(2)
 
+    for c in usend:
+        c.wait_recv()
     dsum = jnp.zeros((C, LANES), f32)
     for j in range(R):
         p = PRE[:, pl.ds(j * LANES, LANES)] + bcol
@@ -290,7 +300,7 @@
         gate = jnp.where(p >= 0.0, 1.0, e) / (1.0 + e)
         act = leakage * p + (1.0 - leakage) * soft
         AIS[:, 0, j] = act.reshape(Pn, SHARE, LANES).astype(bf16)
-        u = RCVW[:, j].astype(f32).reshape(C, LANES)
+        u = RCVU[:, j].astype(f32).reshape(C, LANES)
         d = (u * (leakage + (1.0 - leakage) * gate)).astype(bf16)
         DX[1, 1 + j] = d
         DB[:, pl.ds(j * LANES, LANES)] = d
@@ -369,7 +379,7 @@
     acc = Q1[0]
     for m in range(1, M):
         acc = acc + Q1[m]
-    Q2[block] = acc
+    Q2[block] = acc.astype(bf16)
     heard(1)
     q2send = []
     for k in sorted(range(1, B), key=lambda k: -min(k, B - k)):
@@ -390,9 +400,9 @@
 
     for c in q2send:
         c.wait_recv()
-    acc = Q2[0]
+    acc = Q2[0].astype(f32)
     for m in range(1, B):
-        acc = acc + Q2[m]
+        acc = acc + Q2[m].astype(f32)
     FIN[member] = acc * g.factor
     q3send = []
     for k in range(1, M):
@@ -451,9 +461,11 @@
         pltpu.SMEM((1, SHARE), f32),
         V((2, SHARE * g.H, LANES), f32),
         V((Pn, R + 2, SHARE, LANES), bf16),
-        V((Pn, R + 3 * g.NJ, SHARE, LANES), bf16),
+        V((Pn, R, SHARE, LANES), bf16),
+        V((Pn, 3 * g.NJ, SHARE, LANES), bf16),
         V((Pn, R + 2, SHARE, LANES), bf16),
-        V((Pn, R + 3 * g.NJ, SHARE, LANES), bf16),
+        V((Pn, R, SHARE, LANES), bf16),
+        V((Pn, 3 * g.NJ, SHARE, LANES), bf16),
         V((2, Pn, R + 2, SHARE, LANES), bf16),
         V((9 * C, rows), bf16),
         V((3, R + 2, C, LANES), bf16),
@@ -470,10 +482,10 @@
         V((3, Pn, SHARE, g.KP), bf16),
         V((M, g.T, SHARE, LANES), f32),
         V((M, g.T, SHARE, LANES), f32),
-        V((B, g.T, SHARE, LANES), f32),
+        V((B, g.T, SHARE, LANES), bf16),
         V((M, g.T, SHARE, LANES), f32),
         dma((4,)),
-        *chan, *chan,
+        *chan, *chan, *chan,
         pltpu.SemaphoreType.REGULAR((2,)),
         dma((2, Pn)), dma((2, Pn)),
         dma((8,)), dma((8,)),

time: 51.1 us -> 50.1 us (0.980)
  Pallas kernels: 50.3 us -> 49.3 us
    pallas_call x1, Pallas kernels: 49.5 us -> 48.5 us  [shards(): pl.pallas_call(functools.partial(kernel, g), out_shape=(sds((SHARE, g.H,...]
where the time goes in v7:
time: 50.1 us; the launch traced here: 49.9 us
  Pallas kernels  49.3 us (98%)
  between operations  0.64 us (1%)
    pallas_call x1, Pallas kernels, shards(): pl.pallas_call(functools.partial(kernel, g), out_shape=(sds((SHARE, g.H,...  48.5 us

profile of v7, /device:TPU:1, one launch (start us, length us, event | category | flops | bytes accessed | tf_op | source)
XLA Modules:
  0.0 49.9 jit_solution(10548096243802256776)
XLA Ops:
  0.6 48.5 %shard_map.75 = (bf16[8,48,128]{2,1,0:T(8,128)(2,1)S(1)}, bf16[8,48,128]{2,1,0:T(8,128)(2,1)S(1)}, f32[27,8,64]{2,1,0:T(8,128)S(1)}, f32[1,8]{1,0:T(1,128)S(1)}) custom-call(bf16[8,48,128]{2,1,0:T(8,128)(2,1)} %bitcast.16, bf16[8,48,128]{2,1,0:T(8,128)(2,1)} %bitcast.17, bf16[27,8,64]{2,1,0:T(8,128)(2,1)} %bitcast.18, f32[1,8]{1,0:T(1,128)} %bitcast.19), custom_call_target="tpu_custom_call" | custom-call | tf_op jit(solution)/shard_map/pallas_call | solution.py:498
  49.2 0.7 %shard_map.76 = (bf16[8,48,128]{2,1,0:T(8,128)(2,1)}, bf16[8,48,128]{2,1,0:T(8,128)(2,1)}, f32[27,8,64]{2,1,0:T(8,128)}, f32[1,8]{1,0:T(1,128)}) custom-call(bf16[8,48,128]{2,1,0:T(8,128)(2,1)S(1)} %get-tuple-element.12.act, bf16[8,48,128]{2,1,0:T(8,128)(2,1)S(1)} %get-tuple-element.13.ig, f32[27,8,64]{2,1,0:T(8,128)S(1)} %get-tuple-element.14.wg, ...), custom_call_target="tpu_custom_call" | custom-call | tf_op jit(solution)/shard_map/pallas_call | solution.py:513

commit v8 on v7

--- a/solution.py
+++ b/solution.py
@@ -71,6 +71,13 @@
     def start(c):
         c.start()
         pending.append((None, c))
+
+    def sent_all(copies):
+        for ok, c in copies:
+            if ok is None:
+                c.wait_send()
+            else:
+                pl.when(ok)(c.wait_send)
 
     around = [(ds, dr) for ds in (-1, 0, 1) for dr in (-1, 0, 1) if (ds, dr) != (0, 0)]
 
@@ -381,6 +388,7 @@
         acc = acc + Q1[m]
     Q2[block] = acc.astype(bf16)
     heard(1)
+    early = len(pending)
     q2send = []
     for k in sorted(range(1, B), key=lambda k: -min(k, B - k)):
         c = copy(Q2.at[block], Q2.at[block], q2_s.at[k], q2_r.at[k], block_peer(k), r)
@@ -397,6 +405,8 @@
         start(c)
         isend.append(c)
     AIR[r] = AIS[r]
+    sent_all(pending[:early])
+    del pending[:early]
 
     for c in q2send:
         c.wait_recv()
@@ -429,11 +439,7 @@
     spot = lax.broadcasted_iota(jnp.int32, tile, 0) == lax.broadcasted_iota(jnp.int32, tile, 1)
     bg_o[...] = jnp.sum(jnp.where(spot, sums, 0.0), axis=0, keepdims=True)[:, :SHARE]
 
-    for ok, c in pending:
-        if ok is None:
-            c.wait_send()
-        else:
-            pl.when(ok)(c.wait_send)
+    sent_all(pending)
 
 
 def deliver(act, ig, wg, bg, act_o, ig_o, wg_o, bg_o, sems):

time: 50.1 us -> 50 us (level)
  no operation moved by 1% of the time
where the time goes in v8:
time: 50 us; the launch traced here: 49.8 us
  Pallas kernels  49.2 us (98%)
  between operations  0.64 us (1%)
    pallas_call x1, Pallas kernels, shards(): pl.pallas_call(functools.partial(kernel, g), out_shape=(sds((SHARE, g.H,...  48.4 us

profile of v8, /device:TPU:1, one launch (start us, length us, event | category | flops | bytes accessed | tf_op | source)
XLA Modules:
  0.0 49.8 jit_solution(10969348327605833297)
XLA Ops:
  0.6 48.4 %shard_map.75 = (bf16[8,48,128]{2,1,0:T(8,128)(2,1)S(1)}, bf16[8,48,128]{2,1,0:T(8,128)(2,1)S(1)}, f32[27,8,64]{2,1,0:T(8,128)S(1)}, f32[1,8]{1,0:T(1,128)S(1)}) custom-call(bf16[8,48,128]{2,1,0:T(8,128)(2,1)} %bitcast.16, bf16[8,48,128]{2,1,0:T(8,128)(2,1)} %bitcast.17, bf16[27,8,64]{2,1,0:T(8,128)(2,1)} %bitcast.18, f32[1,8]{1,0:T(1,128)} %bitcast.19), custom_call_target="tpu_custom_call" | custom-call | tf_op jit(solution)/shard_map/pallas_call | solution.py:504
  49.1 0.7 %shard_map.76 = (bf16[8,48,128]{2,1,0:T(8,128)(2,1)}, bf16[8,48,128]{2,1,0:T(8,128)(2,1)}, f32[27,8,64]{2,1,0:T(8,128)}, f32[1,8]{1,0:T(1,128)}) custom-call(bf16[8,48,128]{2,1,0:T(8,128)(2,1)S(1)} %get-tuple-element.12.act, bf16[8,48,128]{2,1,0:T(8,128)(2,1)S(1)} %get-tuple-element.13.ig, f32[27,8,64]{2,1,0:T(8,128)S(1)} %get-tuple-element.14.wg, ...), custom_call_target="tpu_custom_call" | custom-call | tf_op jit(solution)/shard_map/pallas_call | solution.py:519

commit v9 on v8

--- a/solution.py
+++ b/solution.py
@@ -243,16 +243,14 @@
     lane = lax.broadcasted_iota(jnp.int32, (C, LANES), 1)
 
     def spread(row, out, a):
-        def body(i, _):
+        for i in range(R + 2):
             x = row(i).astype(f32).reshape(C, LANES)
-            at = pl.ds(pl.multiple_of(i * LANES, LANES), LANES)
+            at = pl.ds(i * LANES, LANES)
             before = jnp.where(lane == 0, 0.0, pltpu.roll(x, 1, 1))
             after = jnp.where(lane == LANES - 1, 0.0, pltpu.roll(x, LANES - 1, 1))
             out[pl.ds((3 * a) * C, C), at] = before.astype(bf16)
             out[pl.ds((3 * a + 1) * C, C), at] = x.astype(bf16)
             out[pl.ds((3 * a + 2) * C, C), at] = after.astype(bf16)
-            return 0
-        lax.fori_loop(0, R + 2, body, 0)
 
     spread(lambda i: RCVV[:, i], XL, 1)
 
@@ -303,10 +301,7 @@
     for j in range(R):
         p = PRE[:, pl.ds(j * LANES, LANES)] + bcol
         e = jnp.exp(-jnp.abs(p))
-        soft = jnp.maximum(p, 0.0) + jnp.log(1.0 + e)
         gate = jnp.where(p >= 0.0, 1.0, e) / (1.0 + e)
-        act = leakage * p + (1.0 - leakage) * soft
-        AIS[:, 0, j] = act.reshape(Pn, SHARE, LANES).astype(bf16)
         u = RCVU[:, j].astype(f32).reshape(C, LANES)
         d = (u * (leakage + (1.0 - leakage) * gate)).astype(bf16)
         DX[1, 1 + j] = d
@@ -348,6 +343,12 @@
         pl.when(inside(ds, dr))(c.start)
         pending.append((inside(ds, dr), c))
         dcopies.append((inside(-ds, -dr), c))
+
+    for j in range(R):
+        p = PRE[:, pl.ds(j * LANES, LANES)] + bcol
+        soft = jnp.maximum(p, 0.0) + jnp.log(1.0 + jnp.exp(-jnp.abs(p)))
+        act = leakage * p + (1.0 - leakage) * soft
+        AIS[:, 0, j] = act.reshape(Pn, SHARE, LANES).astype(bf16)
 
     for b in range(3):
         whole = W1[2 - b].astype(f32).T

time: 50 us -> 49.9 us (level)
  no operation moved by 1% of the time
where the time goes in v9:
time: 49.9 us; the launch traced here: 49.8 us
  Pallas kernels  49.1 us (98%)
  between operations  0.64 us (1%)
    pallas_call x1, Pallas kernels, shards(): pl.pallas_call(functools.partial(kernel, g), out_shape=(sds((SHARE, g.H,...  48.4 us

profile of v9, /device:TPU:1, one launch (start us, length us, event | category | flops | bytes accessed | tf_op | source)
XLA Modules:
  0.0 49.8 jit_solution(2221379241648691437)
XLA Ops:
  0.6 48.4 %shard_map.75 = (bf16[8,48,128]{2,1,0:T(8,128)(2,1)S(1)}, bf16[8,48,128]{2,1,0:T(8,128)(2,1)S(1)}, f32[27,8,64]{2,1,0:T(8,128)S(1)}, f32[1,8]{1,0:T(1,128)S(1)}) custom-call(bf16[8,48,128]{2,1,0:T(8,128)(2,1)} %bitcast.16, bf16[8,48,128]{2,1,0:T(8,128)(2,1)} %bitcast.17, bf16[27,8,64]{2,1,0:T(8,128)(2,1)} %bitcast.18, f32[1,8]{1,0:T(1,128)} %bitcast.19), custom_call_target="tpu_custom_call" | custom-call | tf_op jit(solution)/shard_map/pallas_call | solution.py:505
  49.0 0.7 %shard_map.76 = (bf16[8,48,128]{2,1,0:T(8,128)(2,1)}, bf16[8,48,128]{2,1,0:T(8,128)(2,1)}, f32[27,8,64]{2,1,0:T(8,128)}, f32[1,8]{1,0:T(1,128)}) custom-call(bf16[8,48,128]{2,1,0:T(8,128)(2,1)S(1)} %get-tuple-element.12.act, bf16[8,48,128]{2,1,0:T(8,128)(2,1)S(1)} %get-tuple-element.13.ig, f32[27,8,64]{2,1,0:T(8,128)S(1)} %get-tuple-element.14.wg, ...), custom_call_target="tpu_custom_call" | custom-call | tf_op jit(solution)/shard_map/pallas_call | solution.py:520

commit v10 on v9

--- a/solution.py
+++ b/solution.py
@@ -367,9 +367,9 @@
             acc = acc + GR[b, q].astype(f32)
         for j in range(g.NJ):
             t = b * g.NJ + j
-            SB[t // g.T, t % g.T] = acc[:, j * LANES : (j + 1) * LANES]
+            SB[t // g.T, t % g.T] = acc[:, j * LANES : (j + 1) * LANES].astype(bf16)
     for t in range(3 * g.NJ, M * g.T):
-        SB[t // g.T, t % g.T] = jnp.zeros(tile, f32)
+        SB[t // g.T, t % g.T] = jnp.zeros(tile, bf16)
     q1send = []
     for k in range(1, M):
         m, to_s = group_peer(k)
@@ -384,9 +384,9 @@
         spread(lambda i, a=a: DX[a, i], DL, a)
     for c in q1send:
         c.wait_recv()
-    acc = Q1[0]
+    acc = Q1[0].astype(f32)
     for m in range(1, M):
-        acc = acc + Q1[m]
+        acc = acc + Q1[m].astype(f32)
     Q2[block] = acc.astype(bf16)
     heard(1)
     early = len(pending)
@@ -487,8 +487,8 @@
         V((3, C, g.KP), f32),
         V((3, Pn, SHARE, g.KP), bf16),
         V((3, Pn, SHARE, g.KP), bf16),
-        V((M, g.T, SHARE, LANES), f32),
-        V((M, g.T, SHARE, LANES), f32),
+        V((M, g.T, SHARE, LANES), bf16),
+        V((M, g.T, SHARE, LANES), bf16),
         V((B, g.T, SHARE, LANES), bf16),
         V((M, g.T, SHARE, LANES), f32),
         dma((4,)),

time: 49.9 us -> 49.7 us (level)
  no operation moved by 1% of the time
where the time goes in v10:
time: 49.7 us; the launch traced here: 49.5 us
  Pallas kernels  48.9 us (98%)
  between operations  0.64 us (1%)
    pallas_call x1, Pallas kernels, shards(): pl.pallas_call(functools.partial(kernel, g), out_shape=(sds((SHARE, g.H,...  48.2 us

profile of v10, /device:TPU:1, one launch (start us, length us, event | category | flops | bytes accessed | tf_op | source)
XLA Modules:
  0.0 49.5 jit_solution(8549313115334860984)
XLA Ops:
  0.6 48.2 %shard_map.75 = (bf16[8,48,128]{2,1,0:T(8,128)(2,1)S(1)}, bf16[8,48,128]{2,1,0:T(8,128)(2,1)S(1)}, f32[27,8,64]{2,1,0:T(8,128)S(1)}, f32[1,8]{1,0:T(1,128)S(1)}) custom-call(bf16[8,48,128]{2,1,0:T(8,128)(2,1)} %bitcast.16, bf16[8,48,128]{2,1,0:T(8,128)(2,1)} %bitcast.17, bf16[27,8,64]{2,1,0:T(8,128)(2,1)} %bitcast.18, f32[1,8]{1,0:T(1,128)} %bitcast.19), custom_call_target="tpu_custom_call" | custom-call | tf_op jit(solution)/shard_map/pallas_call | solution.py:505
  48.8 0.7 %shard_map.76 = (bf16[8,48,128]{2,1,0:T(8,128)(2,1)}, bf16[8,48,128]{2,1,0:T(8,128)(2,1)}, f32[27,8,64]{2,1,0:T(8,128)}, f32[1,8]{1,0:T(1,128)}) custom-call(bf16[8,48,128]{2,1,0:T(8,128)(2,1)S(1)} %get-tuple-element.12.act, bf16[8,48,128]{2,1,0:T(8,128)(2,1)S(1)} %get-tuple-element.13.ig, f32[27,8,64]{2,1,0:T(8,128)S(1)} %get-tuple-element.14.wg, ...), custom_call_target="tpu_custom_call" | custom-call | tf_op jit(solution)/shard_map/pallas_call | solution.py:520
